TPU v7x, 256 devices: a whole 4x4x8 slice. The times are simulated.
256 devices in a mesh: seq: 32 (over z_hi, x, core), head: 8 (over y, z_lo).
Axes of the slice: x: 4, y: 4, z: 8 (z_hi: 4, z_lo: 2; z = z_hi * 2 + z_lo), core: 2. Of those that a mesh axis runs over, the one named last changes fastest.
Arguments:
- queries: bfloat16 [24576, 4096], P('seq', 'head'), may hold values from -100 to 100
- keys: bfloat16 [24576, 4096], P('seq', 'head'), may hold values from -7 to 7
- values: bfloat16 [24576, 4096], P('seq', 'head'), may hold values from -6 to 6
- targets: bfloat16 [24576, 4096], P('seq', 'head'), may hold values from -6 to 6
- token_rate: float32 [24576, 8], P('seq', 'head'), may hold values from 0.1 to 1
- window: int32 [8], P('head'), may hold values from 256 to 512, as said below
- split: int32 [1], replicated, may hold values from 9216 to 15359
- fast_init: float32 [8, 3, 512, 512], P('head'), may hold values from -0.25 to 0.25
Outputs:
- mixed: bfloat16 [24576, 4096], P('seq', 'head')
- fast_final: float32 [8, 3, 512, 512], P('head')
Inputs may be any that keep to these rules, and one draw needn't show every extreme that they name: Some head has a window of exactly 512.
All inputs are finite; a program needn't handle non-finite values.
Results may differ from a plain program's by a relative error of at most 0.0073.
Values may be sent and summed in bfloat16 or wider, within the bound.
No kernel may reach another device: no remote copies, remote signals or barrier semaphores. Data moves between devices by JAX's collectives and lax.ppermute only.
A program may use at most 64 MiB of HBM per device.

v0:
```python
import math

import jax
import jax.numpy as jnp
from jax import lax
from jax.sharding import Mesh
from jax.sharding import PartitionSpec as P

HEADS = 8
HD = 512
HID = 512
WIN = 512
SEQ = ("seq_0", "seq_1", "seq_2")


fast_rate = 0.01
epsilon = 1e-06


def split_up(shard, dim, count):
    before, after = (shard.shape[:dim], shard.shape[dim + 1 :])
    return jnp.moveaxis(shard.reshape(*before, count, -1, *after), dim, 0)


def sent_and_summed(shard, axis, dim):
    count = lax.axis_size(axis)
    pieces = lax.all_to_all(split_up(shard, dim, count), axis, 0, 0, tiled=True)
    return jnp.sum(pieces, axis=0)


def summed_rows(shard, axes, dim):
    far, near = axes
    pieces = split_up(shard, dim, lax.axis_size(far))
    nearer = sent_and_summed(pieces, near, dim + 1)
    arrived = lax.all_to_all(nearer, far, split_axis=0, concat_axis=0, tiled=True)
    return arrived.sum(axis=0)


def rows_for(lines, count):
    spare = -len(lines) % count
    return jnp.pad(lines, [(0, spare)] + [(0, 0)] * (lines.ndim - 1))


def from_everyone(shard, axis):
    copies = jnp.broadcast_to(shard, (lax.axis_size(axis), *shard.shape))
    return lax.all_to_all(copies, axis, split_axis=0, concat_axis=0, tiled=True)


def laid_out(pieces, dim):
    pieces = jnp.moveaxis(pieces, 0, dim)
    shape = pieces.shape
    return pieces.reshape(*shape[:dim], shape[dim] * shape[dim + 1], *shape[dim + 2 :])


def whole_of(shard, axes, dim):
    far, near = axes
    pieces = from_everyone(from_everyone(shard, far), near)
    return laid_out(pieces.swapaxes(0, 1).reshape(-1, *shard.shape), dim)


def nested_sum(shard, axes):
    lines = shard.reshape(-1, shard.shape[-1])
    own = summed_rows(rows_for(lines, lax.axis_size(axes[0]) * lax.axis_size(axes[1])), axes, 0)
    whole = whole_of(own, axes, 0)
    return whole[: len(lines)].reshape(shard.shape)


def taken_together(shard, axis):
    everything = from_everyone(shard, axis)
    return jnp.sum(everything, axis=0)


def shifted(shard, axis, by):
    count = lax.axis_size(axis)
    pairs = [(i, i + by) for i in range(count) if 0 <= i + by < count]
    return lax.ppermute(shard, axis, pairs)


def fast_apply(inputs, weights):
    first = jnp.dot(inputs, weights[0], preferred_element_type=jnp.float32)
    third = jnp.dot(inputs, weights[1], preferred_element_type=jnp.float32)
    act = (jax.nn.silu(first) * third).astype(jnp.bfloat16)
    return lax.dot_general(
        act, weights[2], (((1,), (1,)), ((), ())), preferred_element_type=jnp.float32
    )


def fast_grad(inputs, targets, scaled, weights):
    first = jnp.dot(inputs, weights[0], preferred_element_type=jnp.float32)
    third = jnp.dot(inputs, weights[1], preferred_element_type=jnp.float32)
    sigma = jax.nn.sigmoid(first)
    swish = first * sigma
    act = (swish * third).astype(jnp.bfloat16)
    d_out = (-scaled * targets.astype(jnp.float32)).astype(jnp.bfloat16)
    d_act = jnp.dot(d_out, weights[2], preferred_element_type=jnp.float32)
    d_first = (d_act * third * sigma * (1.0 + first * (1.0 - sigma))).astype(jnp.bfloat16)
    d_third = (d_act * swish).astype(jnp.bfloat16)
    dims = (((0,), (0,)), ((), ()))
    grad_one = lax.dot_general(inputs, d_first, dims, preferred_element_type=jnp.float32)
    grad_three = lax.dot_general(inputs, d_third, dims, preferred_element_type=jnp.float32)
    grad_two = lax.dot_general(d_out, act, dims, preferred_element_type=jnp.float32)
    return jnp.stack([grad_one, grad_three, grad_two])


def attend_head(query_head, key_ext, value_ext, width, anchor):
    local = query_head.shape[0]
    block = math.gcd(local, 512)
    scale = HD ** (-0.5)

    def one_block(start):
        query_block = lax.dynamic_slice_in_dim(query_head, start, block, 0)
        key_block = lax.dynamic_slice_in_dim(key_ext, start, block + WIN, 0)
        value_block = lax.dynamic_slice_in_dim(value_ext, start, block + WIN, 0)
        scores = (
            lax.dot_general(
                query_block, key_block, (((1,), (1,)), ((), ())), preferred_element_type=jnp.float32
            )
            * scale
        )
        query_pos = anchor + start + jnp.arange(block, dtype=jnp.int32)[:, None]
        key_pos = anchor + start - WIN + jnp.arange(block + WIN, dtype=jnp.int32)[None, :]
        live = (key_pos <= query_pos) & (key_pos > query_pos - width) & (key_pos >= 0)
        scores = jnp.where(live, scores, -1e30)
        peak = jnp.max(scores, axis=1, keepdims=True)
        expo = jnp.where(live, jnp.exp(scores - peak), 0.0)
        probs = (expo / jnp.sum(expo, axis=1, keepdims=True)).astype(jnp.bfloat16)
        return jnp.dot(probs, value_block, preferred_element_type=jnp.float32)

    starts = jnp.arange(local // block, dtype=jnp.int32) * block
    return lax.map(one_block, starts).reshape(local, HD)


def renew_weights(weights, grads):
    count = float(HEADS * 3 * HD * HID)
    total = nested_sum(grads, (("seq_0", "seq_1"), "seq_2"))
    square = taken_together(jnp.sum(total * total), "head")
    factor = fast_rate / jnp.sqrt(square / count + epsilon)
    return weights - factor * total


def per_device(queries, keys, values, targets, token_rate, window, split, fast_init):
    local = queries.shape[0]
    anchor = lax.axis_index(SEQ) * local
    reach = -(-WIN // local)
    moved = shifted((keys, values), SEQ, 1)
    key_parts = [moved[0]]
    value_parts = [moved[1]]
    key_ext = jnp.concatenate(key_parts + [keys], axis=0)[reach * local - WIN :]
    value_ext = jnp.concatenate(value_parts + [values], axis=0)[reach * local - WIN :]
    positions = anchor + jnp.arange(local, dtype=jnp.int32)[:, None]
    first_block = (positions < split[0]).astype(jnp.float32)
    second_block = 1.0 - first_block

    def grads_of(weights, mask):
        scaled = token_rate * mask
        pieces = [fast_grad(keys, targets, scaled, weights[0].astype(jnp.bfloat16))]
        return jnp.stack(pieces)

    weights_one = renew_weights(fast_init, grads_of(fast_init, first_block))
    weights_two = renew_weights(weights_one, grads_of(weights_one, second_block))
    attn = attend_head(queries, key_ext, value_ext, window[0], anchor)
    early = fast_apply(queries, fast_init[0].astype(jnp.bfloat16))
    late = fast_apply(queries, weights_one[0].astype(jnp.bfloat16))
    fast_out = first_block * early + second_block * late
    normed = fast_out / jnp.sqrt(jnp.mean(fast_out * fast_out, axis=1, keepdims=True) + epsilon)
    outputs = (attn + normed).astype(jnp.bfloat16)
    return (outputs, weights_two)


def solution(mesh):
    finer = Mesh(
        mesh.devices.reshape(4, 4, 2, mesh.shape["head"]), ("seq_0", "seq_1", "seq_2", "head")
    )
    in_specs = (
        P(SEQ, "head"),
        P(SEQ, "head"),
        P(SEQ, "head"),
        P(SEQ, "head"),
        P(SEQ, "head"),
        P("head"),
        P(),
        P("head", None, None, None),
    )
    out_specs = (P(SEQ, "head"), P("head", None, None, None))
    return jax.shard_map(
        per_device, mesh=finer, in_specs=in_specs, out_specs=out_specs, check_vma=False
    )
```

profile of v0, /device:TPU:1, one launch (start us, length us, event | category | flops | bytes accessed | tf_op | source)
XLA Modules:
  0.0 314.4 jit_solution(3920657562782258865)
XLA Ops:
  0.6 2.2 convert_element_type.71
  8.3 2.4 convolution_bitcast_fusion.4
  13.5 9.1 %all_to_all.52 = f32[2,16,48,512]{3,2,1,0:T(8,128)S(1)} all-to-all(f32[2,16,48,512]{3,2,1,0:T(8,128)S(1)} %bitcast.156), channel_id=1, replica_groups=mesh['seq_0'=4,'seq_1'=4,'seq_2'=2,'head'=8] {'seq_2'}, dimensions={0} | all-to-all | bytes 6291456 | tf_op jit(solution)/shard_map/all_to_all | solution.py:27
  24.2 46.6 %all_to_all.53 = f32[16,48,512]{2,1,0:T(8,128)S(1)} all-to-all(f32[16,48,512]{2,1,0:T(8,128)} %reduce_sum.93), channel_id=1, replica_groups=mesh['seq_0'=4,'seq_1'=4,'seq_2'=2,'head'=8] {'seq_0','seq_1'}, dimensions={0} | all-to-all | bytes 3145728 | tf_op jit(solution)/shard_map/all_to_all | solution.py:35
  71.1 47.5 %all_to_all.54 = f32[16,48,512]{2,1,0:T(8,128)S(1)} all-to-all(f32[16,48,512]{2,1,0:T(8,128)S(1)} %broadcast_in_dim.48), channel_id=1, replica_groups=mesh['seq_0'=4,'seq_1'=4,'seq_2'=2,'head'=8] {'seq_0','seq_1'}, dimensions={0} | all-to-all | bytes 3145728 | tf_op jit(solution)/shard_map/all_to_all | solution.py:46
  119.1 6.4 %all_to_all.55 = f32[2,16,48,512]{3,2,1,0:T(8,128)S(1)} all-to-all(f32[2,16,48,512]{3,2,1,0:T(8,128)S(1)} %broadcast_in_dim.49), channel_id=1, replica_groups=mesh['seq_0'=4,'seq_1'=4,'seq_2'=2,'head'=8] {'seq_2'}, dimensions={0} | all-to-all | bytes 6291456 | tf_op jit(solution)/shard_map/all_to_all | solution.py:46
  127.6 9.1 %all_to_all.56 = f32[8,1,1]{2,1,0:T(1,128)S(1)} all-to-all(f32[8,1,1]{2,1,0:T(1,128)S(1)} %broadcast_in_dim.50), channel_id=1, replica_groups=mesh['seq_0'=4,'seq_1'=4,'seq_2'=2,'head'=8] {'head'}, dimensions={0} | all-to-all | bytes 64 | tf_op jit(solution)/shard_map/all_to_all | solution.py:46
  139.9 2.7 fusion.59
  148.5 8.7 %all_to_all.57 = f32[2,16,48,512]{3,2,1,0:T(8,128)} all-to-all(f32[2,16,48,512]{3,2,1,0:T(8,128)S(1)} %bitcast.157), channel_id=1, replica_groups=mesh['seq_0'=4,'seq_1'=4,'seq_2'=2,'head'=8] {'seq_2'}, dimensions={0} | all-to-all | bytes 6291456 | tf_op jit(solution)/shard_map/all_to_all | solution.py:27
  157.1 3.6 %reduce_sum.98 = f32[16,48,512]{2,1,0:T(8,128)} reduce(f32[2,16,48,512]{3,2,1,0:T(8,128)} %all_to_all.57, f32[]{:T(128)} %constant.86.clone.1), dimensions={0}, to_apply=%region_9.10 | reduce | flops 393216 | bytes 4718596 | tf_op jit(solution)/shard_map/reduce_sum | solution.py:28
  160.7 4.5 %all-to-all-start.6 = ((f32[16,48,512]{2,1,0:T(8,128)}), f32[16,48,512]{2,1,0:T(8,128)}, u32[]{:S(2)}, u32[]{:S(2)}) async-start(f32[16,48,512]{2,1,0:T(8,128)} %reduce_sum.98), calls=%async_computation.6 | async-start | bytes 3145728 | tf_op jit(solution)/shard_map/all_to_all | solution.py:35
  165.2 3.6 %collective-permute-start = (bf16[768,512]{1,0:T(8,128)(2,1)S(1)}, bf16[768,512]{1,0:T(8,128)(2,1)}, u32[]{:S(2)}, u32[]{:S(2)}) collective-permute-start(bf16[768,512]{1,0:T(8,128)(2,1)S(1)} %copy-done.1), channel_id=1, source_target_pairs={{0,8},{8,16},{16,24},{24,32},{32,40},{40,48},{48,56},{56,64},{64,7... | collective-permute-start | bytes 2359304 | tf_op jit(solution)/shard_map/ppermute | solution.py:76
  168.9 1.9 collective-permute-start.1
  172.6 3.7 %fusion.27 = f32[768,512]{0,1:T(8,128)} fusion(f32[768,512]{1,0:T(8,128)} %fusion.33, bf16[768,512]{1,0:T(8,128)(2,1)S(1)} %copy-done.10, bf16[1,3,512,512]{3,2,1,0:T(8,128)(2,1)S(1)} %copy-done.5), kind=kOutput, calls=%fused_computation.71 | convolution fusion | flops 807665664 | bytes 4980736 | tf_op jit(solution)/shard_map/dot_general | solution.py:83
  176.3 4.4 %collective-permute-done = bf16[768,512]{1,0:T(8,128)(2,1)} collective-permute-done((bf16[768,512]{1,0:T(8,128)(2,1)S(1)}, bf16[768,512]{1,0:T(8,128)(2,1)}, u32[]{:S(2)}, u32[]{:S(2)}) %collective-permute-start) | collective-permute-done | bytes 786464 | tf_op jit(solution)/shard_map/ppermute | solution.py:76
  180.7 2.3 pad_maximum_fusion.3
  183.0 11.4 %collective-permute-done.1 = bf16[768,512]{1,0:T(8,128)(2,1)} collective-permute-done((bf16[768,512]{1,0:T(8,128)(2,1)}, bf16[768,512]{1,0:T(8,128)(2,1)}, u32[]{:S(2)}, u32[]{:S(2)}) %collective-permute-start.1) | collective-permute-done | bytes 786464 | tf_op jit(solution)/shard_map/ppermute | solution.py:76
  194.4 2.2 pad_maximum_fusion.2
  196.6 9.9 %all-to-all-done.6 = f32[16,48,512]{2,1,0:T(8,128)} async-done(((f32[16,48,512]{2,1,0:T(8,128)}), f32[16,48,512]{2,1,0:T(8,128)}, u32[]{:S(2)}, u32[]{:S(2)}) %all-to-all-start.6) | async-done | bytes 1572896 | tf_op jit(solution)/shard_map/all_to_all | solution.py:35
  209.4 37.9 %all-to-all-start.7 = ((f32[16,48,512]{2,1,0:T(8,128)}), f32[16,48,512]{2,1,0:T(8,128)}, u32[]{:S(2)}, u32[]{:S(2)}) async-start(f32[16,48,512]{2,1,0:T(8,128)} %broadcast_in_dim.51), calls=%async_computation.7 | async-start | bytes 3145728 | tf_op jit(solution)/shard_map/all_to_all | solution.py:46
  247.3 25.0 %while.12 = (s32[]{:T(128)}, f32[3,256,512]{2,1,0:T(8,128)S(1)}, s32[3]{0:T(128)S(1)}, s32[]{:T(128)}, s32[]{:T(128)}, /*index=5*/bf16[768,512]{1,0:T(8,128)(2,1...) while((s32[]{:T(128)}, f32[3,256,512]{2,1,0:T(8,128)S(1)}, ...), condition=%wide.region_3.4_spmd, body=%wide.region_0.3_spmd.sunk | while | flops 406980864 | bytes 9992992 | solution.py:130
  261.0 1.9 fusion.78
  273.5 2.0 copy.53
  275.5 2.8 fusion.36
  278.3 4.4 %multiply_reduce_fusion.2 = (f32[768]{0:T(1024)S(1)}, f32[768,512]{0,1:T(8,128)}) fusion(bf16[1,3,512,512]{3,2,1,0:T(8,128)(2,1)S(1)} %copy-done.7, f32[512,768]{0,1:T(8,128)} %fusion.36, bf16[768,512]{1,0:T(8,128)(2,1)} %param.10, f32[768]{0:T(1024)S(1)} %broadcast_subtract_fusion.1, f32[768,512]{0,1:T(8,128)} %fusion.27, f32[768]{0:T(1024)S(1)} %fusion.46), kind=kOutput, calls=%fused_computation.55 | convolution fusion | flops 809630976 | bytes 6564864 | tf_op jit(solution)/shard_map/dot_general | solution.py:83
  282.7 2.5 add_convert_fusion
  285.2 3.4 %all-to-all-done.7 = f32[16,48,512]{2,1,0:T(8,128)} async-done(((f32[16,48,512]{2,1,0:T(8,128)}), f32[16,48,512]{2,1,0:T(8,128)}, u32[]{:S(2)}, u32[]{:S(2)}) %all-to-all-start.7) | async-done | bytes 1572896 | tf_op jit(solution)/shard_map/all_to_all | solution.py:46
  290.4 7.4 %all_to_all.58 = f32[2,16,48,512]{3,2,1,0:T(8,128)S(1)} all-to-all(f32[2,16,48,512]{3,2,1,0:T(8,128)S(1)} %broadcast_in_dim.52), channel_id=1, replica_groups=mesh['seq_0'=4,'seq_1'=4,'seq_2'=2,'head'=8] {'seq_2'}, dimensions={0} | all-to-all | bytes 6291456 | tf_op jit(solution)/shard_map/all_to_all | solution.py:46
  300.4 3.3 %all-to-all-start.9 = ((f32[8,1,1]{2,1,0:T(1,128)}), f32[8,1,1]{2,1,0:T(1,128)S(1)}, u32[]{:S(2)}, u32[]{:S(2)}) async-start(f32[8,1,1]{2,1,0:T(1,128)} %broadcast_in_dim.53), calls=%async_computation.9 | async-start | bytes 8192 | tf_op jit(solution)/shard_map/all_to_all | solution.py:46
  303.8 2.3 copy.59
  306.1 2.6 all-to-all-done.9
  312.0 2.4 sub.69
  (97 shorter events, 44.0 us)
Async XLA Ops:
  0.6 2.2 copy-start
  2.8 4.2 %copy-start.4 = (bf16[1,3,512,512]{3,2,1,0:T(8,128)(2,1)}, bf16[1,3,512,512]{3,2,1,0:T(8,128)(2,1)S(1)}, u32[]{:S(2)}) copy-start(bf16[1,3,512,512]{3,2,1,0:T(8,128)(2,1)S(1)} %convert_element_type.71) | copy-start | bytes 4718596
  4.5 2.4 copy-start.17
  4.5 2.4 copy-start.8
  6.9 1.4 copy-start.13
  8.3 2.5 copy-start.14
  138.0 1.9 copy-start.2
  139.9 2.7 copy-start.1
  142.5 1.2 copy-start.6
  143.1 1.1 copy-start.9
  160.7 10.1 %copy-start.5 = (bf16[1,3,512,512]{3,2,1,0:T(8,128)(2,1)S(1)}, bf16[1,3,512,512]{3,2,1,0:T(8,128)(2,1)}, u32[]{:S(2)}) copy-start(bf16[1,3,512,512]{3,2,1,0:T(8,128)(2,1)} %copy-done.4) | copy-start | bytes 4718596
  160.7 10.1 %copy-start.10 = (bf16[768,512]{1,0:T(8,128)(2,1)S(1)}, bf16[768,512]{1,0:T(8,128)(2,1)}, u32[]{:S(2)}) copy-start(bf16[768,512]{1,0:T(8,128)(2,1)} %param.10) | copy-start | bytes 2359300
  160.7 45.8 %all-to-all-start.6 = ((f32[16,48,512]{2,1,0:T(8,128)}), f32[16,48,512]{2,1,0:T(8,128)}, u32[]{:S(2)}, u32[]{:S(2)}) async-start(f32[16,48,512]{2,1,0:T(8,128)} %reduce_sum.98), calls=%async_computation.6 | async-start | bytes 3145728 | tf_op jit(solution)/shard_map/all_to_all | solution.py:35
  165.2 15.5 %collective-permute-start = (bf16[768,512]{1,0:T(8,128)(2,1)S(1)}, bf16[768,512]{1,0:T(8,128)(2,1)}, u32[]{:S(2)}, u32[]{:S(2)}) collective-permute-start(bf16[768,512]{1,0:T(8,128)(2,1)S(1)} %copy-done.1), channel_id=1, source_target_pairs={{0,8},{8,16},{16,24},{24,32},{32,40},{40,48},{48,56},{56,64},{64,7... | collective-permute-start | bytes 2359304 | tf_op jit(solution)/shard_map/ppermute | solution.py:76
  168.9 25.6 %collective-permute-start.1 = (bf16[768,512]{1,0:T(8,128)(2,1)}, bf16[768,512]{1,0:T(8,128)(2,1)}, u32[]{:S(2)}, u32[]{:S(2)}) collective-permute-start(bf16[768,512]{1,0:T(8,128)(2,1)} %param.12), channel_id=1, source_target_pairs={{0,8},{8,16},{16,24},{24,32},{32,40},{40,48},{48,56},{56,64},{64,7... | collective-permute-start | bytes 2359304 | tf_op jit(solution)/shard_map/ppermute | solution.py:76
  176.3 18.1 %copy-start.16 = (bf16[768,512]{1,0:T(8,128)(2,1)S(1)}, bf16[768,512]{1,0:T(8,128)(2,1)}, u32[]{:S(2)}) copy-start(bf16[768,512]{1,0:T(8,128)(2,1)} %param.12) | copy-start | bytes 2359300
  209.4 37.9 %copy-start.11 = (f32[3,256,512]{2,1,0:T(8,128)S(1)}, f32[3,256,512]{2,1,0:T(8,128)}, u32[]{:S(2)}) copy-start(f32[3,256,512]{2,1,0:T(8,128)} %custom-call) | copy-start | bytes 4718596
  209.4 79.2 %all-to-all-start.7 = ((f32[16,48,512]{2,1,0:T(8,128)}), f32[16,48,512]{2,1,0:T(8,128)}, u32[]{:S(2)}, u32[]{:S(2)}) async-start(f32[16,48,512]{2,1,0:T(8,128)} %broadcast_in_dim.51), calls=%async_computation.7 | async-start | bytes 3145728 | tf_op jit(solution)/shard_map/all_to_all | solution.py:46
  252.6 2.3 copy-start.15
  261.0 2.3 copy-start.15
  269.3 2.3 copy-start.15
  272.3 1.1 copy-start.12
  273.5 2.0 copy-start.7
  300.4 8.3 %all-to-all-start.9 = ((f32[8,1,1]{2,1,0:T(1,128)}), f32[8,1,1]{2,1,0:T(1,128)S(1)}, u32[]{:S(2)}, u32[]{:S(2)}) async-start(f32[8,1,1]{2,1,0:T(1,128)} %broadcast_in_dim.53), calls=%async_computation.9 | async-start | bytes 8192 | tf_op jit(solution)/shard_map/all_to_all | solution.py:46
  310.1 1.9 copy-start.3
where the time goes:
time: 316 us; the launch traced here: 314 us
  blocking collectives  135 us (43%)
  starting transfers between devices  51.3 us (16%)
  matrix products  33.1 us (10%)
  waiting for transfers between devices  31.7 us (10%)
  other arithmetic  29.9 us (9%)
  local copies, waits for them, and re-layouts  18.2 us (6%)
  loops' own time  12.2 us (4%)
    all_to_all x4, blocking collectives, from_everyone(): return lax.all_to_all(copies, axis, split_axis=0, concat_axis=0, tiled=True)  70.4 us
    all_to_all x1, blocking collectives, summed_rows(): lax.all_to_all(nearer, far, split_axis=0, concat_axis=0, tiled=True)  46.6 us
    all_to_all x2, starting transfers between devices, from_everyone(): return lax.all_to_all(copies, axis, split_axis=0, concat_axis=0, tiled=True)  41.2 us
    all_to_all x2, blocking collectives, sent_and_summed(): pieces = lax.all_to_all(split_up(shard, dim, count), axis, 0, 0, tiled=True)  17.8 us
    ppermute x2, waiting for transfers between devices, shifted(): return lax.ppermute(shard, axis, pairs)  15.8 us
    another operation x1, loops' own time, attend_head(): return lax.map(one_block, starts).reshape(local, HD)  12.2 us
    all_to_all x1, waiting for transfers between devices, summed_rows(): lax.all_to_all(nearer, far, split_axis=0, concat_axis=0, tiled=True)  9.86 us
    dot_general x2, matrix products, fast_apply(): lax.dot_general(act, weights[2], (((1,), (1,)), ((), ())), preferred_elem...  8.05 us
  transfers between devices with their start and end apart: 5, of which 5 were waited for; matrix products, arithmetic and copies ran while one was open for 12% of the time, Pallas kernels for 0%

commit v1 on v0

v1 whole, which is shorter than its diff:
```python
import math

import jax
import jax.numpy as jnp
from jax import lax
from jax.sharding import Mesh
from jax.sharding import PartitionSpec as P

HEADS = 8
HD = 512
HID = 512
WIN = 512
ROWS = 3 * HD
SEQ = ("z", "x", "core")

fast_rate = 0.01
epsilon = 1e-06
bf16 = jnp.bfloat16
f32 = jnp.float32


def exchange(value, mesh_axes, partner):
    count = math.prod(lax.axis_size(a) for a in mesh_axes)
    return lax.ppermute(value, mesh_axes, [(i, partner(i)) for i in range(count)])


def ring_pair(step):
    def partner(i):
        place, core = divmod(i, 2)
        return (place ^ (1 if core == step else 3)) * 2 + core

    return partner


def swap_x(value, step):
    return exchange(value, ("x", "core"), ring_pair(step))


def swap_z(value, step):
    return exchange(value, ("z", "core"), ring_pair(step))


def swap_core(value):
    return exchange(value, ("core",), lambda i: i ^ 1)


def swap_head(value, bits):
    return exchange(value, ("head",), lambda i: i ^ bits)


def part(value, index):
    half = value.shape[0] // 2
    return lax.dynamic_slice_in_dim(value, index * half, half, 0)


def joined(own, other, bit):
    half = own.shape[0]
    whole = jnp.zeros((2 * half, own.shape[1]), own.dtype)
    whole = lax.dynamic_update_slice_in_dim(whole, own, bit * half, 0)
    return lax.dynamic_update_slice_in_dim(whole, other, (1 - bit) * half, 0)


def summed_over_seq(grad):
    core = lax.axis_index("core")
    place = lax.axis_index("x")
    low, high = place & 1, place >> 1
    first = jnp.where(core == 0, low ^ high, high)
    second = jnp.where(core == 0, high, low ^ high)

    got = swap_core(part(grad, 1 - core).astype(bf16))
    own = part(grad, core)
    got_x = swap_x((part(own, 1 - first) + part(got, 1 - first).astype(f32)).astype(bf16), 0)
    own = part(own, first) + part(got, first).astype(f32)
    got_x2 = swap_x((part(own, 1 - second) + part(got_x, 1 - second).astype(f32)).astype(bf16), 1)
    own = part(own, second) + part(got_x, second).astype(f32) + got_x2.astype(f32)
    for step in range(2):
        own = own.astype(bf16)
        own = own.astype(f32) + swap_z(own, step).astype(f32)

    square = jnp.broadcast_to(jnp.sum(own * own), (8, 128))
    square = square + swap_head(square, 2)
    square = square + swap_head(square, 6)
    square = square + swap_head(square, 1)
    square = square + swap_x(square, 1)
    square = square + swap_x(square, 0)
    square = square + swap_core(square)

    total = own.astype(bf16)
    total = joined(total, swap_x(total, 1), second)
    total = joined(total, swap_x(total, 0), first)
    total = joined(total, swap_core(total), core)
    return total, square[0, 0]


def fast_apply(inputs, weights):
    first = jnp.dot(inputs, weights[0], preferred_element_type=f32)
    third = jnp.dot(inputs, weights[1], preferred_element_type=f32)
    act = (jax.nn.silu(first) * third).astype(bf16)
    return lax.dot_general(act, weights[2], (((1,), (1,)), ((), ())), preferred_element_type=f32)


def fast_grad(inputs, targets, scaled, weights):
    first = jnp.dot(inputs, weights[0], preferred_element_type=f32)
    third = jnp.dot(inputs, weights[1], preferred_element_type=f32)
    sigma = jax.nn.sigmoid(first)
    swish = first * sigma
    act = (swish * third).astype(bf16)
    d_out = (-scaled * targets.astype(f32)).astype(bf16)
    d_act = jnp.dot(d_out, weights[2], preferred_element_type=f32)
    d_first = (d_act * third * sigma * (1.0 + first * (1.0 - sigma))).astype(bf16)
    d_third = (d_act * swish).astype(bf16)
    dims = (((0,), (0,)), ((), ()))
    grad_one = lax.dot_general(inputs, d_first, dims, preferred_element_type=f32)
    grad_three = lax.dot_general(inputs, d_third, dims, preferred_element_type=f32)
    grad_two = lax.dot_general(d_out, act, dims, preferred_element_type=f32)
    return jnp.concatenate([grad_one, grad_three, grad_two], axis=0)


def attend_head(query_head, key_ext, value_ext, width, anchor):
    local = query_head.shape[0]
    block = math.gcd(local, 512)
    scale = HD ** (-0.5)
    done = []
    for start in range(0, local, block):
        query_block = query_head[start : start + block]
        key_block = key_ext[start : start + block + WIN]
        value_block = value_ext[start : start + block + WIN]
        scores = lax.dot_general(query_block, key_block, (((1,), (1,)), ((), ())), preferred_element_type=f32) * scale
        query_pos = anchor + start + jnp.arange(block, dtype=jnp.int32)[:, None]
        key_pos = anchor + start - WIN + jnp.arange(block + WIN, dtype=jnp.int32)[None, :]
        live = (key_pos <= query_pos) & (key_pos > query_pos - width) & (key_pos >= 0)
        scores = jnp.where(live, scores, -1e30)
        peak = jnp.max(scores, axis=1, keepdims=True)
        expo = jnp.where(live, jnp.exp(scores - peak), 0.0)
        probs = (expo / jnp.sum(expo, axis=1, keepdims=True)).astype(bf16)
        done.append(jnp.dot(probs, value_block, preferred_element_type=f32))
    return jnp.concatenate(done, axis=0)


def per_device(queries, keys, values, targets, token_rate, window, split, fast_init):
    local = queries.shape[0]
    anchor = lax.axis_index(SEQ) * local
    count = lax.axis_size(SEQ)
    onward = [(i, i + 1) for i in range(count - 1)]
    key_ext = jnp.concatenate([lax.ppermute(keys[local - WIN :], SEQ, onward), keys], axis=0)
    value_ext = jnp.concatenate([lax.ppermute(values[local - WIN :], SEQ, onward), values], axis=0)
    positions = anchor + jnp.arange(local, dtype=jnp.int32)[:, None]
    first_block = (positions < split[0]).astype(f32)
    second_block = 1.0 - first_block

    def renewed(weights, mask):
        grad = fast_grad(keys, targets, token_rate * mask, weights.reshape(3, HD, HID).astype(bf16))
        total, square = summed_over_seq(grad)
        factor = fast_rate / jnp.sqrt(square / float(HEADS * ROWS * HID) + epsilon)
        return weights - factor * total.astype(f32)

    weights_zero = fast_init.reshape(ROWS, HID)
    weights_one = renewed(weights_zero, first_block)
    weights_two = renewed(weights_one, second_block)
    attn = attend_head(queries, key_ext, value_ext, window[0], anchor)
    early = fast_apply(queries, weights_zero.reshape(3, HD, HID).astype(bf16))
    late = fast_apply(queries, weights_one.reshape(3, HD, HID).astype(bf16))
    fast_out = first_block * early + second_block * late
    normed = fast_out / jnp.sqrt(jnp.mean(fast_out * fast_out, axis=1, keepdims=True) + epsilon)
    outputs = (attn + normed).astype(bf16)
    return (outputs, weights_two.reshape(1, 3, HD, HID))


def solution(mesh):
    finer = Mesh(mesh.devices.reshape(4, 4, 2, mesh.shape["head"]), ("z", "x", "core", "head"))
    tokens = P(SEQ, "head")
    weights = P("head", None, None, None)
    return jax.shard_map(
        per_device,
        mesh=finer,
        in_specs=(tokens,) * 5 + (P("head"), P(), weights),
        out_specs=(tokens, weights),
        check_vma=False,
    )
```

time: 316 us -> 200 us (0.63)
  blocking collectives: 135 us -> 0 us
  waiting for transfers between devices: 31.7 us -> 53 us
  loops' own time: 12.2 us -> 0 us
  starting transfers between devices: 51.3 us -> 60 us
  other arithmetic: 29.9 us -> 21.8 us
  local copies, waits for them, and re-layouts: 18.2 us -> 23.6 us
  matrix products: 33.1 us -> 37.1 us
    all_to_all x7 -> x0, blocking collectives: 135 us -> none  [the longest x4 70.4 us: from_everyone(): return lax.all_to_all(copies, axis, split_axis=0, concat_axis=0, tiled=True)]
    ppermute x2 -> x30, starting transfers between devices: 5.55 us -> 60 us  [the longest x28 54.9 us: exchange(): lax.ppermute(value, mesh_axes, [(i, partner(i)) for i in range(count)])]
    all_to_all x3 -> x0, starting transfers between devices: 45.7 us -> none  [the longest x2 41.2 us: from_everyone(): return lax.all_to_all(copies, axis, split_axis=0, concat_axis=0, tiled=True)]
    ppermute x2 -> x30, waiting for transfers between devices: 15.8 us -> 53 us  [the longest x28 53 us: exchange(): lax.ppermute(value, mesh_axes, [(i, partner(i)) for i in range(count)])]
    all_to_all x3 -> x0, waiting for transfers between devices: 15.9 us -> none  [the longest x1 9.86 us: summed_rows(): lax.all_to_all(nearer, far, split_axis=0, concat_axis=0, tiled=True)]
    another operation x1 -> x0, loops' own time: 12.2 us -> none  [attend_head(): return lax.map(one_block, starts).reshape(local, HD)]
    reduce_sum x11 -> x5, other arithmetic: 12.2 us -> 2.57 us  [the longest x2 1.54 us: summed_over_seq(): square = jnp.broadcast_to(jnp.sum(own * own), (8, 128))]
    dynamic_update_slice x0 -> x10, local copies, waits for them, and re-layouts: none -> 8.14 us  [the longest x4 4.18 us: joined(): whole = lax.dynamic_update_slice_in_dim(whole, own, bit * half, 0)]
  transfers between devices with their start and end apart: 5 -> 30, of which waited for: 5 -> 17; matrix products, arithmetic and copies ran while one was open for 12% -> 28% of each run, Pallas kernels for 0% -> 0%
where the time goes in v1:
time: 200 us; the launch traced here: 199 us
  starting transfers between devices  60 us (30%)
  waiting for transfers between devices  53 us (26%)
  matrix products  37.1 us (19%)
  local copies, waits for them, and re-layouts  23.6 us (12%)
  other arithmetic  21.8 us (11%)
  between operations  3.96 us (2%)
    ppermute x28, starting transfers between devices, exchange(): lax.ppermute(value, mesh_axes, [(i, partner(i)) for i in range(count)])  54.9 us
    ppermute x28, waiting for transfers between devices, exchange(): lax.ppermute(value, mesh_axes, [(i, partner(i)) for i in range(count)])  53 us
    dot_general x2, matrix products, fast_apply(): lax.dot_general(act, weights[2], (((1,), (1,)), ((), ())), preferred_elem...  8.57 us
    unnamed x40, local copies, waits for them, and re-layouts  7.95 us
    dot_general x3, matrix products, attend_head(): done.append(jnp.dot(probs, value_block, preferred_element_type=f32))  6.37 us
    dot_general x2, matrix products, fast_apply(): first = jnp.dot(inputs, weights[0], preferred_element_type=f32)  5.6 us
    dynamic_update_slice x4, local copies, waits for them, and re-layouts, joined(): whole = lax.dynamic_update_slice_in_dim(whole, own, bit * half, 0)  4.18 us
  transfers between devices with their start and end apart: 30, of which 17 were waited for; matrix products, arithmetic and copies ran while one was open for 28% of the time, Pallas kernels for 0%

profile of v1, /device:TPU:1, one launch (start us, length us, event | category | flops | bytes accessed | tf_op | source)
XLA Modules:
  0.0 199.5 jit_solution(5650526846648174705)
XLA Ops:
  0.6 2.2 %convert_element_type.173 = bf16[1,3,512,512]{3,2,1,0:T(8,128)(2,1)S(1)} convert(f32[1,3,512,512]{3,2,1,0:T(8,128)} %param.15) | non-fusion elementwise | flops 786432 | bytes 4718592 | tf_op jit(solution)/shard_map/convert_element_type | solution.py:161
  18.0 3.3 %collective-permute-start.2 = (bf16[768,512]{1,0:T(8,128)(2,1)S(1)}, bf16[768,512]{1,0:T(8,128)(2,1)}, u32[]{:S(2)}, u32[]{:S(2)}) collective-permute-start(bf16[768,512]{1,0:T(8,128)(2,1)S(1)} %dynamic-slice_convert_fusion.1), channel_id=1, source_target_pairs={{0,8},{8,0},{1,9},{9,1},{2,10},{10,2},{3,11},{11,3},{4,12},{12,4},... | collective-permute-start | bytes 2359304 | tf_op jit(solution)/shard_map/ppermute | solution.py:24
  26.9 3.2 %collective-permute-start = (bf16[512,512]{1,0:T(8,128)(2,1)}, bf16[512,512]{1,0:T(8,128)(2,1)}, u32[]{:S(2)}, u32[]{:S(2)}) collective-permute-start(bf16[512,512]{1,0:T(8,128)(2,1)} %slice.63), channel_id=1, source_target_pairs={{0,8},{8,16},{16,24},{24,32},{32,40},{40,48},{48,56},{56,64},{64,7... | collective-permute-start | bytes 1572872 | tf_op jit(solution)/shard_map/ppermute | solution.py:145
  34.3 2.8 %fusion.39 = f32[768,512]{1,0:T(8,128)} fusion(bf16[768,512]{1,0:T(8,128)(2,1)} %param.8, bf16[1,3,512,512]{3,2,1,0:T(8,128)(2,1)S(1)} %convert_element_type.173), kind=kOutput, calls=%fused_computation.85 | convolution fusion | flops 402653184 | bytes 2883584 | tf_op jit(solution)/shard_map/dot_general | solution.py:96
  37.2 6.9 %collective-permute-done.4 = bf16[192,512]{1,0:T(8,128)(2,1)S(1)} collective-permute-done((bf16[192,512]{1,0:T(8,128)(2,1)S(1)}, bf16[192,512]{1,0:T(8,128)(2,1)S(1)}, u32[]{:S(2)}, u32[]{:S(2)}) %collective-permute-start.4) | collective-permute-done | bytes 196640 | tf_op jit(solution)/shard_map/ppermute | solution.py:24
  45.1 5.7 %collective-permute-start.5 = (bf16[192,512]{1,0:T(8,128)(2,1)S(1)}, bf16[192,512]{1,0:T(8,128)(2,1)S(1)}, u32[]{:S(2)}, u32[]{:S(2)}) collective-permute-start(bf16[192,512]{1,0:T(8,128)(2,1)S(1)} %add_convert_fusion.6), channel_id=1, source_target_pairs={{0,64},{8,200},{64,0},{72,136},{128,192},{136,72},{192,128},{200,8... | collective-permute-start | bytes 589832 | tf_op jit(solution)/shard_map/ppermute | solution.py:24
  50.8 3.9 %fusion.22 = f32[768,512]{1,0:T(8,128)} fusion(f32[768,512]{1,0:T(8,128)} %fusion.39, bf16[768,512]{1,0:T(8,128)(2,1)} %param.8, bf16[1,3,512,512]{3,2,1,0:T(8,128)(2,1)S(1)} %convert_element_type.173), kind=kOutput, calls=%fused_computation.54 | convolution fusion | flops 807665664 | bytes 4980736 | tf_op jit(solution)/shard_map/dot_general | solution.py:99
  57.3 5.7 %collective-permute-done.6 = bf16[192,512]{1,0:T(8,128)(2,1)S(1)} collective-permute-done((bf16[192,512]{1,0:T(8,128)(2,1)S(1)}, bf16[192,512]{1,0:T(8,128)(2,1)S(1)}, u32[]{:S(2)}, u32[]{:S(2)}) %collective-permute-start.6) | collective-permute-done | bytes 196640 | tf_op jit(solution)/shard_map/ppermute | solution.py:24
  63.1 3.2 %collective-permute-start.13 = (bf16[192,512]{1,0:T(8,128)(2,1)S(1)}, bf16[192,512]{1,0:T(8,128)(2,1)S(1)}, u32[]{:S(2)}, u32[]{:S(2)}) collective-permute-start(bf16[192,512]{1,0:T(8,128)(2,1)S(1)} %get-tuple-element.7), channel_id=1, source_target_pairs={{0,48},{8,24},{16,32},{24,8},{32,16},{40,56},{48,0},{56,40},{1,49}... | collective-permute-start | bytes 589832 | tf_op jit(solution)/shard_map/ppermute | solution.py:24
  69.3 2.4 %collective-permute-start.7 = (f32[8,128]{1,0:T(8,128)S(1)}, f32[8,128]{1,0:T(8,128)S(1)}, u32[]{:S(2)}, u32[]{:S(2)}) collective-permute-start(f32[8,128]{1,0:T(8,128)S(1)} %broadcast_in_dim.17), channel_id=1, source_target_pairs={{0,2},{1,3},{2,0},{3,1},{4,6},{5,7},{6,4},{7,5},{8,10},{9,11},{10,... | collective-permute-start | bytes 12296 | tf_op jit(solution)/shard_map/ppermute | solution.py:24
  71.7 6.0 %collective-permute-start.14 = (bf16[384,512]{1,0:T(8,128)(2,1)S(1)}, bf16[384,512]{1,0:T(8,128)(2,1)S(1)}, u32[]{:S(2)}, u32[]{:S(2)}) collective-permute-start(bf16[384,512]{1,0:T(8,128)(2,1)S(1)} %constant_dynamic-update-slice_fusion.11), channel_id=1, source_target_pairs={{0,16},{8,56},{16,0},{24,40},{32,48},{40,24},{48,32},{56,8},{1,17}... | collective-permute-start | bytes 1179656 | tf_op jit(solution)/shard_map/ppermute | solution.py:24
  78.7 3.0 %collective-permute-start.8 = (f32[8,128]{1,0:T(8,128)S(1)}, f32[8,128]{1,0:T(8,128)S(1)}, u32[]{:S(2)}, u32[]{:S(2)}) collective-permute-start(f32[8,128]{1,0:T(8,128)S(1)} %broadcast_add_fusion.1), channel_id=1, source_target_pairs={{0,6},{1,7},{2,4},{3,5},{4,2},{5,3},{6,0},{7,1},{8,14},{9,15},{10,... | collective-permute-start | bytes 12296 | tf_op jit(solution)/shard_map/ppermute | solution.py:24
  84.2 2.6 %collective-permute-start.15 = (bf16[768,512]{1,0:T(8,128)(2,1)}, bf16[768,512]{1,0:T(8,128)(2,1)}, u32[]{:S(2)}, u32[]{:S(2)}) collective-permute-start(bf16[768,512]{1,0:T(8,128)(2,1)} %constant_dynamic-update-slice_fusion.9), channel_id=1, source_target_pairs={{0,8},{8,0},{1,9},{9,1},{2,10},{10,2},{3,11},{11,3},{4,12},{12,4},... | collective-permute-start | bytes 2359304 | tf_op jit(solution)/shard_map/ppermute | solution.py:24
  87.6 2.4 %collective-permute-done.9 = f32[8,128]{1,0:T(8,128)S(1)} collective-permute-done((f32[8,128]{1,0:T(8,128)S(1)}, f32[8,128]{1,0:T(8,128)S(1)}, u32[]{:S(2)}, u32[]{:S(2)}) %collective-permute-start.9) | collective-permute-done | bytes 4128 | tf_op jit(solution)/shard_map/ppermute | solution.py:24
  90.1 2.4 %collective-permute-done.10 = f32[8,128]{1,0:T(8,128)S(1)} collective-permute-done((f32[8,128]{1,0:T(8,128)S(1)}, f32[8,128]{1,0:T(8,128)S(1)}, u32[]{:S(2)}, u32[]{:S(2)}) %collective-permute-start.10) | collective-permute-done | bytes 4128 | tf_op jit(solution)/shard_map/ppermute | solution.py:24
  93.6 2.6 %collective-permute-done.11 = f32[8,128]{1,0:T(8,128)S(1)} collective-permute-done((f32[8,128]{1,0:T(8,128)S(1)}, f32[8,128]{1,0:T(8,128)S(1)}, u32[]{:S(2)}, u32[]{:S(2)}) %collective-permute-start.11) | collective-permute-done | bytes 4128 | tf_op jit(solution)/shard_map/ppermute | solution.py:24
  96.2 3.5 %collective-permute-start.12 = (f32[8,128]{1,0:T(8,128)S(1)}, f32[8,128]{1,0:T(8,128)S(1)}, u32[]{:S(2)}, u32[]{:S(2)}) collective-permute-start(f32[8,128]{1,0:T(8,128)S(1)} %add.339), channel_id=1, source_target_pairs={{0,8},{8,0},{1,9},{9,1},{2,10},{10,2},{3,11},{11,3},{4,12},{12,4},... | collective-permute-start | bytes 12296 | tf_op jit(solution)/shard_map/ppermute | solution.py:24
  114.6 3.2 %fusion.59 = f32[256,512]{1,0:T(8,128)} fusion(bf16[768,512]{1,0:T(8,128)(2,1)} %param.10, f32[256,768]{0,1:T(8,128)} %copy-done.17, f32[256]{0:T(256)S(1)} %fusion.37, f32[256]{0:T(256)S(1)} %get-tuple-element.12, s32[256]{0:T(256)S(1)} %get-tuple-element.25, s32[256]{0:T(256)S(1)} %get-tuple-element.24, s32[768]{0:T(1024)S(1)} %iota_add_fusion, ...), kind=kOutput, calls=%fused_computation.114 | convolution fusion | flops 202899456 | bytes 2105088 | tf_op jit(solution)/shard_map/dot_general | solution.py:136
  123.4 5.2 %collective-permute-done.17 = bf16[384,512]{1,0:T(8,128)(2,1)S(1)} collective-permute-done((bf16[384,512]{1,0:T(8,128)(2,1)S(1)}, bf16[384,512]{1,0:T(8,128)(2,1)S(1)}, u32[]{:S(2)}, u32[]{:S(2)}) %collective-permute-start.17) | collective-permute-done | bytes 393248 | tf_op jit(solution)/shard_map/ppermute | solution.py:24
  129.2 4.4 %collective-permute-done.18 = bf16[192,512]{1,0:T(8,128)(2,1)S(1)} collective-permute-done((bf16[192,512]{1,0:T(8,128)(2,1)S(1)}, bf16[192,512]{1,0:T(8,128)(2,1)S(1)}, u32[]{:S(2)}, u32[]{:S(2)}) %collective-permute-start.18) | collective-permute-done | bytes 196640 | tf_op jit(solution)/shard_map/ppermute | solution.py:24
  133.6 6.2 %collective-permute-start.19 = (bf16[192,512]{1,0:T(8,128)(2,1)S(1)}, bf16[192,512]{1,0:T(8,128)(2,1)S(1)}, u32[]{:S(2)}, u32[]{:S(2)}) collective-permute-start(bf16[192,512]{1,0:T(8,128)(2,1)S(1)} %add_convert_fusion.3), channel_id=1, source_target_pairs={{0,64},{8,200},{64,0},{72,136},{128,192},{136,72},{192,128},{200,8... | collective-permute-start | bytes 589832 | tf_op jit(solution)/shard_map/ppermute | solution.py:24
  141.4 2.7 %collective-permute-done.19 = bf16[192,512]{1,0:T(8,128)(2,1)S(1)} collective-permute-done((bf16[192,512]{1,0:T(8,128)(2,1)S(1)}, bf16[192,512]{1,0:T(8,128)(2,1)S(1)}, u32[]{:S(2)}, u32[]{:S(2)}) %collective-permute-start.19) | collective-permute-done | bytes 196640 | tf_op jit(solution)/shard_map/ppermute | solution.py:24
  145.1 7.0 %collective-permute-done.20 = bf16[192,512]{1,0:T(8,128)(2,1)S(1)} collective-permute-done((bf16[192,512]{1,0:T(8,128)(2,1)S(1)}, bf16[192,512]{1,0:T(8,128)(2,1)S(1)}, u32[]{:S(2)}, u32[]{:S(2)}) %collective-permute-start.20) | collective-permute-done | bytes 196640 | tf_op jit(solution)/shard_map/ppermute | solution.py:24
  156.7 2.2 %collective-permute-start.22 = (f32[8,128]{1,0:T(8,128)S(1)}, f32[8,128]{1,0:T(8,128)S(1)}, u32[]{:S(2)}, u32[]{:S(2)}) collective-permute-start(f32[8,128]{1,0:T(8,128)S(1)} %broadcast_add_fusion), channel_id=1, source_target_pairs={{0,6},{1,7},{2,4},{3,5},{4,2},{5,3},{6,0},{7,1},{8,14},{9,15},{10,... | collective-permute-start | bytes 12296 | tf_op jit(solution)/shard_map/ppermute | solution.py:24
  161.2 2.4 %collective-permute-done.27 = bf16[192,512]{1,0:T(8,128)(2,1)S(1)} collective-permute-done((bf16[192,512]{1,0:T(8,128)(2,1)S(1)}, bf16[192,512]{1,0:T(8,128)(2,1)S(1)}, u32[]{:S(2)}, u32[]{:S(2)}) %collective-permute-start.27) | collective-permute-done | bytes 196640 | tf_op jit(solution)/shard_map/ppermute | solution.py:24
  165.4 2.8 %fusion.49 = f32[512,768]{0,1:T(8,128)} fusion(bf16[768,512]{1,0:T(8,128)(2,1)S(1)} %copy-done.12, bf16[1536,512]{1,0:T(8,128)(2,1)} %copy-done.9), kind=kOutput, calls=%fused_computation.94 | convolution fusion | flops 402653184 | bytes 2883584 | tf_op jit(solution)/shard_map/dot_general | solution.py:96
  169.8 3.9 %collective-permute-done.28 = bf16[384,512]{1,0:T(8,128)(2,1)S(1)} collective-permute-done((bf16[384,512]{1,0:T(8,128)(2,1)S(1)}, bf16[384,512]{1,0:T(8,128)(2,1)S(1)}, u32[]{:S(2)}, u32[]{:S(2)}) %collective-permute-start.28) | collective-permute-done | bytes 393248 | tf_op jit(solution)/shard_map/ppermute | solution.py:24
  174.5 7.2 %collective-permute-start.29 = (bf16[768,512]{1,0:T(8,128)(2,1)}, bf16[768,512]{1,0:T(8,128)(2,1)}, u32[]{:S(2)}, u32[]{:S(2)}) collective-permute-start(bf16[768,512]{1,0:T(8,128)(2,1)} %constant_dynamic-update-slice_fusion.14), channel_id=1, source_target_pairs={{0,8},{8,0},{1,9},{9,1},{2,10},{10,2},{3,11},{11,3},{4,12},{12,4},... | collective-permute-start | bytes 2359304 | tf_op jit(solution)/shard_map/ppermute | solution.py:24
  181.7 4.7 %multiply_reduce_fusion = (f32[768]{0:T(1024)S(1)}, f32[768,512]{1,0:T(8,128)}) fusion(bf16[1536,512]{1,0:T(8,128)(2,1)} %copy-done.9, f32[512,768]{0,1:T(8,128)} %fusion.49, bf16[768,512]{1,0:T(8,128)(2,1)} %param.8, f32[768]{0:T(1024)S(1)} %broadcast_subtract_fusion, f32[768,512]{1,0:T(8,128)} %fusion.22, f32[768]{0:T(1024)S(1)} %compare_convert_fusion.1), kind=kOutput, calls=%fused_computation.33 | convolution fusion | flops 809630976 | bytes 6562816 | tf_op jit(solution)/shard_map/dot_general | solution.py:99
  187.0 3.2 %collective-permute-done.25 = f32[8,128]{1,0:T(8,128)S(1)} collective-permute-done((f32[8,128]{1,0:T(8,128)S(1)}, f32[8,128]{1,0:T(8,128)S(1)}, u32[]{:S(2)}, u32[]{:S(2)}) %collective-permute-start.25) | collective-permute-done | bytes 4128 | tf_op jit(solution)/shard_map/ppermute | solution.py:24
  190.2 3.0 %fusion.3 = bf16[768,512]{1,0:T(8,128)(2,1)} fusion(f32[256,512]{1,0:T(8,128)} %fusion.59, f32[256,512]{1,0:T(8,128)} %fusion.26, f32[256,512]{1,0:T(8,128)} %fusion.29, f32[768,512]{1,0:T(8,128)} %get-tuple-element.19, f32[768]{0:T(1024)S(1)} %add_sqrt_fusion), kind=kLoop, calls=%fused_computation.10 | loop fusion | flops 1966080 | bytes 3935232 | tf_op jit(solution)/shard_map/convert_element_type | solution.py:165
  197.1 2.4 %multiply_subtract_fusion = f32[1536,512]{1,0:T(8,128)} fusion(bf16[1536,512]{1,0:T(8,128)(2,1)S(1)} %constant_dynamic-update-slice_fusion.5, bf16[1536,512]{1,0:T(8,128)(2,1)S(1)} %copy-done.5, f32[1,3,512,512]{3,2,1,0:T(8,128)S(1)} %copy-done, f32[]{:T(128)} %bitcast.17, f32[]{:T(128)} %bitcast.10), kind=kLoop, calls=%fused_computation.3 | loop fusion | flops 4718592 | bytes 9437192 | tf_op jit(solution)/shard_map/sub | solution.py:155
  (161 shorter events, 73.3 us)
Async XLA Ops:
  18.0 5.4 %collective-permute-start.2 = (bf16[768,512]{1,0:T(8,128)(2,1)S(1)}, bf16[768,512]{1,0:T(8,128)(2,1)}, u32[]{:S(2)}, u32[]{:S(2)}) collective-permute-start(bf16[768,512]{1,0:T(8,128)(2,1)S(1)} %dynamic-slice_convert_fusion.1), channel_id=1, source_target_pairs={{0,8},{8,0},{1,9},{9,1},{2,10},{10,2},{3,11},{11,3},{4,12},{12,4},... | collective-permute-start | bytes 2359304 | tf_op jit(solution)/shard_map/ppermute | solution.py:24
  21.3 8.7 %copy-start.13 = (bf16[768,512]{1,0:T(8,128)(2,1)S(1)}, bf16[768,512]{1,0:T(8,128)(2,1)}, u32[]{:S(2)}) copy-start(bf16[768,512]{1,0:T(8,128)(2,1)} %param.10) | copy-start | bytes 2359300
  25.2 8.0 %collective-permute-start.3 = (bf16[384,512]{1,0:T(8,128)(2,1)S(1)}, bf16[384,512]{1,0:T(8,128)(2,1)}, u32[]{:S(2)}, u32[]{:S(2)}) collective-permute-start(bf16[384,512]{1,0:T(8,128)(2,1)S(1)} %get-tuple-element.10), channel_id=1, source_target_pairs={{0,16},{8,56},{16,0},{24,40},{32,48},{40,24},{48,32},{56,8},{1,17}... | collective-permute-start | bytes 1179656 | tf_op jit(solution)/shard_map/ppermute | solution.py:24
  26.9 90.9 %collective-permute-start = (bf16[512,512]{1,0:T(8,128)(2,1)}, bf16[512,512]{1,0:T(8,128)(2,1)}, u32[]{:S(2)}, u32[]{:S(2)}) collective-permute-start(bf16[512,512]{1,0:T(8,128)(2,1)} %slice.63), channel_id=1, source_target_pairs={{0,8},{8,16},{16,24},{24,32},{32,40},{40,48},{48,56},{56,64},{64,7... | collective-permute-start | bytes 1572872 | tf_op jit(solution)/shard_map/ppermute | solution.py:145
  30.9 90.9 %collective-permute-start.1 = (bf16[512,512]{1,0:T(8,128)(2,1)}, bf16[512,512]{1,0:T(8,128)(2,1)}, u32[]{:S(2)}, u32[]{:S(2)}) collective-permute-start(bf16[512,512]{1,0:T(8,128)(2,1)} %slice.66), channel_id=1, source_target_pairs={{0,8},{8,16},{16,24},{24,32},{32,40},{40,48},{48,56},{56,64},{64,7... | collective-permute-start | bytes 1572872 | tf_op jit(solution)/shard_map/ppermute | solution.py:146
  34.2 9.9 %collective-permute-start.4 = (bf16[192,512]{1,0:T(8,128)(2,1)S(1)}, bf16[192,512]{1,0:T(8,128)(2,1)S(1)}, u32[]{:S(2)}, u32[]{:S(2)}) collective-permute-start(bf16[192,512]{1,0:T(8,128)(2,1)S(1)} %add_convert_fusion.7), channel_id=1, source_target_pairs={{0,48},{8,24},{16,32},{24,8},{32,16},{40,56},{48,0},{56,40},{1,49}... | collective-permute-start | bytes 589832 | tf_op jit(solution)/shard_map/ppermute | solution.py:24
  45.1 10.2 %collective-permute-start.5 = (bf16[192,512]{1,0:T(8,128)(2,1)S(1)}, bf16[192,512]{1,0:T(8,128)(2,1)S(1)}, u32[]{:S(2)}, u32[]{:S(2)}) collective-permute-start(bf16[192,512]{1,0:T(8,128)(2,1)S(1)} %add_convert_fusion.6), channel_id=1, source_target_pairs={{0,64},{8,200},{64,0},{72,136},{128,192},{136,72},{192,128},{200,8... | collective-permute-start | bytes 589832 | tf_op jit(solution)/shard_map/ppermute | solution.py:24
  55.4 7.6 %collective-permute-start.6 = (bf16[192,512]{1,0:T(8,128)(2,1)S(1)}, bf16[192,512]{1,0:T(8,128)(2,1)S(1)}, u32[]{:S(2)}, u32[]{:S(2)}) collective-permute-start(bf16[192,512]{1,0:T(8,128)(2,1)S(1)} %add_convert_fusion.5), channel_id=1, source_target_pairs={{0,192},{8,72},{64,128},{72,8},{128,64},{136,200},{192,0},{200,136... | collective-permute-start | bytes 589832 | tf_op jit(solution)/shard_map/ppermute | solution.py:24
  63.1 8.6 %collective-permute-start.13 = (bf16[192,512]{1,0:T(8,128)(2,1)S(1)}, bf16[192,512]{1,0:T(8,128)(2,1)S(1)}, u32[]{:S(2)}, u32[]{:S(2)}) collective-permute-start(bf16[192,512]{1,0:T(8,128)(2,1)S(1)} %get-tuple-element.7), channel_id=1, source_target_pairs={{0,48},{8,24},{16,32},{24,8},{32,16},{40,56},{48,0},{56,40},{1,49}... | collective-permute-start | bytes 589832 | tf_op jit(solution)/shard_map/ppermute | solution.py:24
  67.7 15.7 %copy-start.17 = (f32[256,768]{0,1:T(8,128)}, f32[256,768]{0,1:T(8,128)S(1)}, u32[]{:S(2)}) copy-start(f32[256,768]{0,1:T(8,128)S(1)} %get-tuple-element.13) | copy-start | bytes 2359300
  69.3 8.7 %collective-permute-start.7 = (f32[8,128]{1,0:T(8,128)S(1)}, f32[8,128]{1,0:T(8,128)S(1)}, u32[]{:S(2)}, u32[]{:S(2)}) collective-permute-start(f32[8,128]{1,0:T(8,128)S(1)} %broadcast_in_dim.17), channel_id=1, source_target_pairs={{0,2},{1,3},{2,0},{3,1},{4,6},{5,7},{6,4},{7,5},{8,10},{9,11},{10,... | collective-permute-start | bytes 12296 | tf_op jit(solution)/shard_map/ppermute | solution.py:24
  71.7 11.7 %collective-permute-start.14 = (bf16[384,512]{1,0:T(8,128)(2,1)S(1)}, bf16[384,512]{1,0:T(8,128)(2,1)S(1)}, u32[]{:S(2)}, u32[]{:S(2)}) collective-permute-start(bf16[384,512]{1,0:T(8,128)(2,1)S(1)} %constant_dynamic-update-slice_fusion.11), channel_id=1, source_target_pairs={{0,16},{8,56},{16,0},{24,40},{32,48},{40,24},{48,32},{56,8},{1,17}... | collective-permute-start | bytes 1179656 | tf_op jit(solution)/shard_map/ppermute | solution.py:24
  78.7 8.1 %collective-permute-start.8 = (f32[8,128]{1,0:T(8,128)S(1)}, f32[8,128]{1,0:T(8,128)S(1)}, u32[]{:S(2)}, u32[]{:S(2)}) collective-permute-start(f32[8,128]{1,0:T(8,128)S(1)} %broadcast_add_fusion.1), channel_id=1, source_target_pairs={{0,6},{1,7},{2,4},{3,5},{4,2},{5,3},{6,0},{7,1},{8,14},{9,15},{10,... | collective-permute-start | bytes 12296 | tf_op jit(solution)/shard_map/ppermute | solution.py:24
  84.2 19.1 %collective-permute-start.15 = (bf16[768,512]{1,0:T(8,128)(2,1)}, bf16[768,512]{1,0:T(8,128)(2,1)}, u32[]{:S(2)}, u32[]{:S(2)}) collective-permute-start(bf16[768,512]{1,0:T(8,128)(2,1)} %constant_dynamic-update-slice_fusion.9), channel_id=1, source_target_pairs={{0,8},{8,0},{1,9},{9,1},{2,10},{10,2},{3,11},{11,3},{4,12},{12,4},... | collective-permute-start | bytes 2359304 | tf_op jit(solution)/shard_map/ppermute | solution.py:24
  87.5 2.5 %collective-permute-start.9 = (f32[8,128]{1,0:T(8,128)S(1)}, f32[8,128]{1,0:T(8,128)S(1)}, u32[]{:S(2)}, u32[]{:S(2)}) collective-permute-start(f32[8,128]{1,0:T(8,128)S(1)} %fusion.109), channel_id=1, source_target_pairs={{0,1},{1,0},{2,3},{3,2},{4,5},{5,4},{6,7},{7,6},{8,9},{9,8},{10,11... | collective-permute-start | bytes 12296 | tf_op jit(solution)/shard_map/ppermute | solution.py:24
  90.0 2.5 %collective-permute-start.10 = (f32[8,128]{1,0:T(8,128)S(1)}, f32[8,128]{1,0:T(8,128)S(1)}, u32[]{:S(2)}, u32[]{:S(2)}) collective-permute-start(f32[8,128]{1,0:T(8,128)S(1)} %add.337), channel_id=1, source_target_pairs={{0,48},{8,24},{16,32},{24,8},{32,16},{40,56},{48,0},{56,40},{1,49}... | collective-permute-start | bytes 12296 | tf_op jit(solution)/shard_map/ppermute | solution.py:24
  92.5 3.7 %collective-permute-start.11 = (f32[8,128]{1,0:T(8,128)S(1)}, f32[8,128]{1,0:T(8,128)S(1)}, u32[]{:S(2)}, u32[]{:S(2)}) collective-permute-start(f32[8,128]{1,0:T(8,128)S(1)} %add.338), channel_id=1, source_target_pairs={{0,16},{8,56},{16,0},{24,40},{32,48},{40,24},{48,32},{56,8},{1,17}... | collective-permute-start | bytes 12296 | tf_op jit(solution)/shard_map/ppermute | solution.py:24
  96.2 4.3 %collective-permute-start.12 = (f32[8,128]{1,0:T(8,128)S(1)}, f32[8,128]{1,0:T(8,128)S(1)}, u32[]{:S(2)}, u32[]{:S(2)}) collective-permute-start(f32[8,128]{1,0:T(8,128)S(1)} %add.339), channel_id=1, source_target_pairs={{0,8},{8,0},{1,9},{9,1},{2,10},{10,2},{3,11},{11,3},{4,12},{12,4},... | collective-permute-start | bytes 12296 | tf_op jit(solution)/shard_map/ppermute | solution.py:24
  114.2 4.9 %collective-permute-start.16 = (bf16[768,512]{1,0:T(8,128)(2,1)}, bf16[768,512]{1,0:T(8,128)(2,1)}, u32[]{:S(2)}, u32[]{:S(2)}) collective-permute-start(bf16[768,512]{1,0:T(8,128)(2,1)} %dynamic-slice_convert_fusion), channel_id=1, source_target_pairs={{0,8},{8,0},{1,9},{9,1},{2,10},{10,2},{3,11},{11,3},{4,12},{12,4},... | collective-permute-start | bytes 2359304 | tf_op jit(solution)/shard_map/ppermute | solution.py:24
  120.7 7.9 %collective-permute-start.17 = (bf16[384,512]{1,0:T(8,128)(2,1)S(1)}, bf16[384,512]{1,0:T(8,128)(2,1)S(1)}, u32[]{:S(2)}, u32[]{:S(2)}) collective-permute-start(bf16[384,512]{1,0:T(8,128)(2,1)S(1)} %get-tuple-element.8), channel_id=1, source_target_pairs={{0,16},{8,56},{16,0},{24,40},{32,48},{40,24},{48,32},{56,8},{1,17}... | collective-permute-start | bytes 1179656 | tf_op jit(solution)/shard_map/ppermute | solution.py:24
  128.6 4.9 %collective-permute-start.18 = (bf16[192,512]{1,0:T(8,128)(2,1)S(1)}, bf16[192,512]{1,0:T(8,128)(2,1)S(1)}, u32[]{:S(2)}, u32[]{:S(2)}) collective-permute-start(bf16[192,512]{1,0:T(8,128)(2,1)S(1)} %add_convert_fusion.4), channel_id=1, source_target_pairs={{0,48},{8,24},{16,32},{24,8},{32,16},{40,56},{48,0},{56,40},{1,49}... | collective-permute-start | bytes 589832 | tf_op jit(solution)/shard_map/ppermute | solution.py:24
  133.6 10.5 %collective-permute-start.19 = (bf16[192,512]{1,0:T(8,128)(2,1)S(1)}, bf16[192,512]{1,0:T(8,128)(2,1)S(1)}, u32[]{:S(2)}, u32[]{:S(2)}) collective-permute-start(bf16[192,512]{1,0:T(8,128)(2,1)S(1)} %add_convert_fusion.3), channel_id=1, source_target_pairs={{0,64},{8,200},{64,0},{72,136},{128,192},{136,72},{192,128},{200,8... | collective-permute-start | bytes 589832 | tf_op jit(solution)/shard_map/ppermute | solution.py:24
  144.2 8.0 %collective-permute-start.20 = (bf16[192,512]{1,0:T(8,128)(2,1)S(1)}, bf16[192,512]{1,0:T(8,128)(2,1)S(1)}, u32[]{:S(2)}, u32[]{:S(2)}) collective-permute-start(bf16[192,512]{1,0:T(8,128)(2,1)S(1)} %add_convert_fusion.2), channel_id=1, source_target_pairs={{0,192},{8,72},{64,128},{72,8},{128,64},{136,200},{192,0},{200,136... | collective-permute-start | bytes 589832 | tf_op jit(solution)/shard_map/ppermute | solution.py:24
  153.5 2.5 %collective-permute-start.21 = (f32[8,128]{1,0:T(8,128)S(1)}, f32[8,128]{1,0:T(8,128)S(1)}, u32[]{:S(2)}, u32[]{:S(2)}) collective-permute-start(f32[8,128]{1,0:T(8,128)S(1)} %broadcast_in_dim.34), channel_id=1, source_target_pairs={{0,2},{1,3},{2,0},{3,1},{4,6},{5,7},{6,4},{7,5},{8,10},{9,11},{10,... | collective-permute-start | bytes 12296 | tf_op jit(solution)/shard_map/ppermute | solution.py:24
  156.7 3.8 %collective-permute-start.22 = (f32[8,128]{1,0:T(8,128)S(1)}, f32[8,128]{1,0:T(8,128)S(1)}, u32[]{:S(2)}, u32[]{:S(2)}) collective-permute-start(f32[8,128]{1,0:T(8,128)S(1)} %broadcast_add_fusion), channel_id=1, source_target_pairs={{0,6},{1,7},{2,4},{3,5},{4,2},{5,3},{6,0},{7,1},{8,14},{9,15},{10,... | collective-permute-start | bytes 12296 | tf_op jit(solution)/shard_map/ppermute | solution.py:24
  159.1 4.6 %collective-permute-start.27 = (bf16[192,512]{1,0:T(8,128)(2,1)S(1)}, bf16[192,512]{1,0:T(8,128)(2,1)S(1)}, u32[]{:S(2)}, u32[]{:S(2)}) collective-permute-start(bf16[192,512]{1,0:T(8,128)(2,1)S(1)} %get-tuple-element.5), channel_id=1, source_target_pairs={{0,48},{8,24},{16,32},{24,8},{32,16},{40,56},{48,0},{56,40},{1,49}... | collective-permute-start | bytes 589832 | tf_op jit(solution)/shard_map/ppermute | solution.py:24
  161.1 7.0 %collective-permute-start.23 = (f32[8,128]{1,0:T(8,128)S(1)}, f32[8,128]{1,0:T(8,128)S(1)}, u32[]{:S(2)}, u32[]{:S(2)}) collective-permute-start(f32[8,128]{1,0:T(8,128)S(1)} %fusion.108), channel_id=1, source_target_pairs={{0,1},{1,0},{2,3},{3,2},{4,5},{5,4},{6,7},{7,6},{8,9},{9,8},{10,11... | collective-permute-start | bytes 12296 | tf_op jit(solution)/shard_map/ppermute | solution.py:24
  163.7 10.0 %collective-permute-start.28 = (bf16[384,512]{1,0:T(8,128)(2,1)S(1)}, bf16[384,512]{1,0:T(8,128)(2,1)S(1)}, u32[]{:S(2)}, u32[]{:S(2)}) collective-permute-start(bf16[384,512]{1,0:T(8,128)(2,1)S(1)} %constant_dynamic-update-slice_fusion.13), channel_id=1, source_target_pairs={{0,16},{8,56},{16,0},{24,40},{32,48},{40,24},{48,32},{56,8},{1,17}... | collective-permute-start | bytes 1179656 | tf_op jit(solution)/shard_map/ppermute | solution.py:24
  168.1 18.3 %collective-permute-start.24 = (f32[8,128]{1,0:T(8,128)S(1)}, f32[8,128]{1,0:T(8,128)S(1)}, u32[]{:S(2)}, u32[]{:S(2)}) collective-permute-start(f32[8,128]{1,0:T(8,128)S(1)} %add.358), channel_id=1, source_target_pairs={{0,48},{8,24},{16,32},{24,8},{32,16},{40,56},{48,0},{56,40},{1,49}... | collective-permute-start | bytes 12296 | tf_op jit(solution)/shard_map/ppermute | solution.py:24
  174.5 21.4 %collective-permute-start.29 = (bf16[768,512]{1,0:T(8,128)(2,1)}, bf16[768,512]{1,0:T(8,128)(2,1)}, u32[]{:S(2)}, u32[]{:S(2)}) collective-permute-start(bf16[768,512]{1,0:T(8,128)(2,1)} %constant_dynamic-update-slice_fusion.14), channel_id=1, source_target_pairs={{0,8},{8,0},{1,9},{9,1},{2,10},{10,2},{3,11},{11,3},{4,12},{12,4},... | collective-permute-start | bytes 2359304 | tf_op jit(solution)/shard_map/ppermute | solution.py:24
  186.5 3.8 %collective-permute-start.25 = (f32[8,128]{1,0:T(8,128)S(1)}, f32[8,128]{1,0:T(8,128)S(1)}, u32[]{:S(2)}, u32[]{:S(2)}) collective-permute-start(f32[8,128]{1,0:T(8,128)S(1)} %add.359), channel_id=1, source_target_pairs={{0,16},{8,56},{16,0},{24,40},{32,48},{40,24},{48,32},{56,8},{1,17}... | collective-permute-start | bytes 12296 | tf_op jit(solution)/shard_map/ppermute | solution.py:24
  190.2 3.0 %collective-permute-start.26 = (f32[8,128]{1,0:T(8,128)S(1)}, f32[8,128]{1,0:T(8,128)S(1)}, u32[]{:S(2)}, u32[]{:S(2)}) collective-permute-start(f32[8,128]{1,0:T(8,128)S(1)} %add.360), channel_id=1, source_target_pairs={{0,8},{8,0},{1,9},{9,1},{2,10},{10,2},{3,11},{11,3},{4,12},{12,4},... | collective-permute-start | bytes 12296 | tf_op jit(solution)/shard_map/ppermute | solution.py:24
  (17 other events, 39.3 us)

commit v2 on v1

v2 whole, which is shorter than its diff:
```python
import functools
import math

import jax
import jax.numpy as jnp
from jax import lax
from jax.experimental import pallas as pl
from jax.experimental.pallas import tpu as pltpu
from jax.sharding import Mesh
from jax.sharding import PartitionSpec as P

HEADS = 8
HD = 512
HID = 512
WIN = 512
ROWS = 3 * HD
SEQ = ("z", "x", "core")
TILE = 256

fast_rate = 0.01
epsilon = 1e-06
bf16 = jnp.bfloat16
f32 = jnp.float32
VMEM_SPEC = pl.BlockSpec(memory_space=pltpu.VMEM)
SMEM_SPEC = pl.BlockSpec(memory_space=pltpu.SMEM)
PARAMS = pltpu.CompilerParams(vmem_limit_bytes=48 << 20)


def dot(a, b, over_a, over_b):
    return lax.dot_general(a, b, (((over_a,), (over_b,)), ((), ())), preferred_element_type=f32)


def exchange(value, mesh_axes, partner):
    count = math.prod(lax.axis_size(a) for a in mesh_axes)
    return lax.ppermute(value, mesh_axes, [(i, partner(i)) for i in range(count)])


def ring_pair(step):
    def partner(i):
        place, core = divmod(i, 2)
        return (place ^ (1 if core == step else 3)) * 2 + core

    return partner


def swap_x(value, step):
    return exchange(value, ("x", "core"), ring_pair(step))


def swap_z(value, step):
    return exchange(value, ("z", "core"), ring_pair(step))


def swap_core(value):
    return exchange(value, ("core",), lambda i: i ^ 1)


def swap_head(value, bits):
    return exchange(value, ("head",), lambda i: i ^ bits)


def of_four(value, swap):
    return (value + swap(value, 1)) + (swap(value, 2) + swap(value, 3))


def summed_squares(value):
    square = jnp.broadcast_to(jnp.sum(value * value), (8, 128))
    square = square + swap_core(square)
    square = of_four(square, lambda v, k: swap_head(v, 2 * k))
    square = of_four(square, lambda v, k: exchange(v, ("x",), lambda i: i ^ k))
    square = square + swap_head(square, 1)
    return square[0, 0].reshape(1)


def part(value, index):
    half = value.shape[0] // 2
    return lax.dynamic_slice_in_dim(value, index * half, half, 0)


def halves():
    core = lax.axis_index("core")
    place = lax.axis_index("x")
    low, high = place & 1, place >> 1
    first = jnp.where(core == 0, low ^ high, high)
    second = jnp.where(core == 0, high, low ^ high)
    return core, first, second


def piece_starts():
    core, a, b = halves()
    here = [(a, b), (a, 1 - b), (1 - a, b), (1 - a, 1 - b)]
    there = [(b, a), (b, 1 - a), (1 - b, a), (1 - b, 1 - a)]
    places = [core * 4 + i * 2 + j for i, j in here] + [(1 - core) * 4 + i * 2 + j for i, j in there]
    return (jnp.stack(places) * (ROWS // 8)).astype(jnp.int32)


def reduced(sent, own, beside=None):
    _, first, second = halves()
    got = swap_core(sent)
    got_x = swap_x((part(own, 1 - first) + part(got, 1 - first).astype(f32)).astype(bf16), 0)
    own = part(own, first) + part(got, first).astype(f32)
    got_x2 = swap_x((part(own, 1 - second) + part(got_x, 1 - second).astype(f32)).astype(bf16), 1)
    own = part(own, second) + part(got_x, second).astype(f32) + got_x2.astype(f32)
    own = own.astype(bf16)
    other = swap_z(own, 0)
    done = None
    if beside is not None:
        done, other = beside(own, other)
    own = (own.astype(f32) + other.astype(f32)).astype(bf16)
    return own.astype(f32) + swap_z(own, 1).astype(f32), done


def gathered(own):
    near = swap_x(own, 1)
    far = swap_x(own, 0)
    both = swap_x(near, 0)
    here = [own, near, far, both]
    return here + [swap_core(v) for v in here]


def grads(place, keys_ref, targets_ref, rate_ref, wb_ref, grad_ref, send_ref, keep_ref):
    keys = keys_ref[...]
    first = dot(keys, wb_ref[0:HD], 1, 0)
    third = dot(keys, wb_ref[HD : 2 * HD], 1, 0)
    d_out = (-rate_ref[...] * targets_ref[...].astype(f32)).astype(bf16)
    d_act = dot(d_out, wb_ref[2 * HD :], 1, 0)
    sigma = jax.nn.sigmoid(first)
    swish = first * sigma
    act = (swish * third).astype(bf16)
    d_first = (d_act * third * sigma * (1.0 + first * (1.0 - sigma))).astype(bf16)
    d_third = (d_act * swish).astype(bf16)
    grad_ref[0:HD] = dot(keys, d_first, 0, 0)
    grad_ref[HD : 2 * HD] = dot(keys, d_third, 0, 0)
    grad_ref[2 * HD :] = dot(d_out, act, 0, 0)
    half = ROWS // 2
    send_ref[...] = grad_ref[pl.ds(pl.multiple_of((1 - place) * half, half), half)].astype(bf16)
    keep_ref[...] = grad_ref[pl.ds(pl.multiple_of(place * half, half), half)]


def first_kernel(place_ref, keys_ref, targets_ref, rate_ref, w_ref, wb_ref, send_ref, keep_ref, grad_ref):
    wb_ref[...] = w_ref[...].astype(bf16)
    grads(place_ref[0], keys_ref, targets_ref, rate_ref, wb_ref, grad_ref, send_ref, keep_ref)


def renew(starts_ref, square_ref, w_ref, pieces, new_ref, wb_ref=None):
    mean = jnp.full((1, HID), square_ref[0] / float(HEADS * ROWS * HID), f32)
    factor = fast_rate / jnp.sqrt(mean + epsilon)
    rows = ROWS // 8
    for i, piece in enumerate(pieces):
        at = pl.ds(pl.multiple_of(starts_ref[i], rows), rows)
        new = w_ref[at] - factor * piece[...].astype(f32)
        new_ref[at] = new
        if wb_ref is not None:
            wb_ref[at] = new.astype(bf16)


def second_kernel(place_ref, starts_ref, square_ref, keys_ref, targets_ref, rate_ref, w_ref, *rest):
    pieces, (new_ref, wb_ref, send_ref, keep_ref, grad_ref) = rest[:8], rest[8:]
    renew(starts_ref, square_ref, w_ref, pieces, new_ref, wb_ref)
    grads(place_ref[0], keys_ref, targets_ref, rate_ref, wb_ref, grad_ref, send_ref, keep_ref)


def last_kernel(starts_ref, square_ref, w_ref, *rest):
    renew(starts_ref, square_ref, w_ref, rest[:8], rest[8])


def attend_kernel(meta_ref, q_ref, halo_k_ref, k_ref, halo_v_ref, v_ref, out_ref):
    local = q_ref.shape[0]
    anchor, width = meta_ref[0], meta_ref[1]
    scale = HD ** (-0.5)
    for start in range(0, local, TILE):
        spans = []
        if start < WIN:
            spans.append((halo_k_ref, halo_v_ref, start, WIN, start - WIN))
        spans.append((k_ref, v_ref, max(start - WIN, 0), start + TILE, 0))
        query = q_ref[start : start + TILE]
        scores = []
        for keys, _, low, high, base in spans:
            s = dot(query, keys[low:high], 1, 1) * scale
            row = lax.broadcasted_iota(jnp.int32, s.shape, 0) + start
            col = lax.broadcasted_iota(jnp.int32, s.shape, 1) + (low - WIN if base else low)
            live = (col <= row) & (col > row - width) & (col >= -anchor)
            scores.append(jnp.where(live, s, -1e30))
        peak = functools.reduce(jnp.maximum, [jnp.max(s, axis=1, keepdims=True) for s in scores])
        expo = [jnp.exp(s - peak) for s in scores]
        total = sum(jnp.sum(e, axis=1, keepdims=True) for e in expo)
        inverse = 1.0 / total
        attn = 0.0
        for e, (_, values, low, high, _) in zip(expo, spans):
            attn = attn + dot((e * inverse).astype(bf16), values[low:high], 1, 0)
        out_ref[start : start + TILE] = attn


def apply_kernel(meta_ref, q_ref, attn_ref, early_ref, late_ref, out_ref, y_ref):
    anchor, split = meta_ref[0], meta_ref[2]

    def fast(query, wb_ref):
        first = dot(query, wb_ref[0:HD], 1, 0)
        third = dot(query, wb_ref[HD : 2 * HD], 1, 0)
        act = (first * jax.nn.sigmoid(first) * third).astype(bf16)
        return dot(act, wb_ref[2 * HD :], 1, 1)

    for start in range(0, q_ref.shape[0], TILE):
        rows = slice(start, start + TILE)

        @pl.when(anchor + start < split)
        def _():
            y_ref[...] = fast(q_ref[rows], early_ref)

        @pl.when(anchor + start + TILE > split)
        def _():
            late = fast(q_ref[rows], late_ref)
            position = anchor + start + lax.broadcasted_iota(jnp.int32, late.shape, 0)
            y_ref[...] = jnp.where(position < split, y_ref[...], late)

        y = y_ref[...]
        norm = y / jnp.sqrt(jnp.mean(y * y, axis=1, keepdims=True) + epsilon)
        out_ref[rows] = (attn_ref[rows] + norm).astype(bf16)


def call(kernel, specs, outs, args, scratch=()):
    return pl.pallas_call(
        kernel,
        out_shape=outs,
        in_specs=specs,
        out_specs=jax.tree.map(lambda _: VMEM_SPEC, outs),
        scratch_shapes=list(scratch),
        compiler_params=PARAMS,
    )(*args)


def array(shape, dtype):
    return jax.ShapeDtypeStruct(shape, dtype)


def per_device(queries, keys, values, targets, token_rate, window, split, fast_init):
    local = queries.shape[0]
    anchor = lax.axis_index(SEQ) * local
    count = lax.axis_size(SEQ)
    onward = [(i, i + 1) for i in range(count - 1)]
    halo_k = lax.ppermute(keys[local - WIN :], SEQ, onward)
    halo_v = lax.ppermute(values[local - WIN :], SEQ, onward)
    positions = anchor + jnp.arange(local, dtype=jnp.int32)[:, None]
    first_block = (positions < split[0]).astype(f32)
    rate_zero = token_rate * first_block
    rate_one = token_rate * (1.0 - first_block)
    core = lax.axis_index("core").astype(jnp.int32).reshape(1)
    starts = piece_starts()
    meta = jnp.stack([anchor, window[0], split[0]]).astype(jnp.int32)
    weights_zero = fast_init.reshape(ROWS, HID)
    half = ROWS // 2
    wide = [array((half, HID), bf16), array((half, HID), f32)]
    scratch = [pltpu.VMEM((ROWS, HID), f32)]

    wb_zero, sent, own = call(
        first_kernel,
        [SMEM_SPEC] + [VMEM_SPEC] * 4,
        [array((ROWS, HID), bf16)] + wide,
        (core, keys, targets, rate_zero, weights_zero),
        scratch,
    )

    def attend(before, after):
        query, _ = lax.optimization_barrier((queries, before))
        attn = call(
            attend_kernel,
            [SMEM_SPEC] + [VMEM_SPEC] * 5,
            array((local, HD), f32),
            (meta, query, halo_k, keys, halo_v, values),
        )
        return lax.optimization_barrier((attn, after))

    total, attn = reduced(sent, own, attend)
    square = summed_squares(total)
    pieces = gathered(total.astype(bf16))
    weights_one, wb_one, sent, own = call(
        second_kernel,
        [SMEM_SPEC] * 3 + [VMEM_SPEC] * 12,
        [array((ROWS, HID), f32), array((ROWS, HID), bf16)] + wide,
        (core, starts, square, keys, targets, rate_one, weights_zero, *pieces),
        scratch,
    )

    def apply(before, after):
        query, _ = lax.optimization_barrier((queries, before))
        outputs = call(
            apply_kernel,
            [SMEM_SPEC] + [VMEM_SPEC] * 4,
            array((local, HD), bf16),
            (meta, query, attn, wb_zero, wb_one),
            [pltpu.VMEM((TILE, HD), f32)],
        )
        return lax.optimization_barrier((outputs, after))

    total, outputs = reduced(sent, own, apply)
    square = summed_squares(total)
    pieces = gathered(total.astype(bf16))
    weights_two = call(
        last_kernel,
        [SMEM_SPEC] * 2 + [VMEM_SPEC] * 9,
        array((ROWS, HID), f32),
        (starts, square, weights_one, *pieces),
    )
    return (outputs, weights_two.reshape(1, 3, HD, HID))


def solution(mesh):
    finer = Mesh(mesh.devices.reshape(4, 4, 2, mesh.shape["head"]), ("z", "x", "core", "head"))
    tokens = P(SEQ, "head")
    weights = P("head", None, None, None)
    return jax.shard_map(
        per_device,
        mesh=finer,
        in_specs=(tokens,) * 5 + (P("head"), P(), weights),
        out_specs=(tokens, weights),
        check_vma=False,
    )
```

time: 200 us -> 180 us (0.900)
  matrix products: 37.1 us -> 0 us
  Pallas kernels: 0 us -> 24 us
  starting transfers between devices: 60 us -> 77 us
  local copies, waits for them, and re-layouts: 23.6 us -> 13.6 us
  other arithmetic: 21.8 us -> 12.1 us
  waiting for transfers between devices: 53 us -> 49.9 us
    dot_general x22 -> x0, matrix products: 37.1 us -> none  [the longest x2 8.57 us: fast_apply(): lax.dot_general(act, weights[2], (((1,), (1,)), ((), ())), preferred_elem...]
    pallas_call x0 -> x5, Pallas kernels: none -> 24 us  [call(): pl.pallas_call(kernel, out_shape=outs, in_specs=specs, out_specs=jax.tree...]
    ppermute x28 -> x40, starting transfers between devices: 54.9 us -> 71.3 us  [exchange(): lax.ppermute(value, mesh_axes, [(i, partner(i)) for i in range(count)])]
    dynamic_update_slice x10 -> x0, local copies, waits for them, and re-layouts: 8.14 us -> none  [the longest x4 4.18 us: joined(): whole = lax.dynamic_update_slice_in_dim(whole, own, bit * half, 0)]
    ppermute x28 -> x40, waiting for transfers between devices: 53 us -> 49.4 us  [exchange(): lax.ppermute(value, mesh_axes, [(i, partner(i)) for i in range(count)])]
    convert_element_type x12 -> x10, other arithmetic: 11.5 us -> 7.99 us  [the longest x2 3.76 us: reduced(): (part(own, 1 - first) + part(got, 1 - first).astype(f32)).astype(bf16)]
    reduce_sum x5 -> x0, other arithmetic: 2.57 us -> none  [the longest x2 1.54 us: summed_over_seq(): square = jnp.broadcast_to(jnp.sum(own * own), (8, 128))]
    concatenate x2 -> x0, other arithmetic: 2.47 us -> none  [fast_grad(): return jnp.concatenate([grad_one, grad_three, grad_two], axis=0)]
  transfers between devices with their start and end apart: 30 -> 42, of which waited for: 17 -> 18; matrix products, arithmetic and copies ran while one was open for 28% -> 4% of each run, Pallas kernels for 0% -> 4%
where the time goes in v2:
time: 180 us; the launch traced here: 179 us
  starting transfers between devices  77 us (43%)
  waiting for transfers between devices  49.9 us (28%)
  Pallas kernels  24 us (13%)
  local copies, waits for them, and re-layouts  13.6 us (8%)
  other arithmetic  12.1 us (7%)
  between operations  2.36 us (1%)
    ppermute x40, starting transfers between devices, exchange(): lax.ppermute(value, mesh_axes, [(i, partner(i)) for i in range(count)])  71.3 us
    ppermute x40, waiting for transfers between devices, exchange(): lax.ppermute(value, mesh_axes, [(i, partner(i)) for i in range(count)])  49.4 us
    pallas_call x5, Pallas kernels, call(): pl.pallas_call(kernel, out_shape=outs, in_specs=specs, out_specs=jax.tree...  24 us
    unnamed x33, local copies, waits for them, and re-layouts  8.89 us
    convert_element_type x2, other arithmetic, reduced(): (part(own, 1 - first) + part(got, 1 - first).astype(f32)).astype(bf16)  3.76 us
  transfers between devices with their start and end apart: 42, of which 18 were waited for; matrix products, arithmetic and copies ran while one was open for 4% of the time, Pallas kernels for 4%

profile of v2, /device:TPU:1, one launch (start us, length us, event | category | flops | bytes accessed | tf_op | source)
XLA Modules:
  0.0 178.9 jit_solution(17001225184704720860)
XLA Ops:
  2.4 6.0 %shard_map.95 = (bf16[1536,512]{1,0:T(8,128)(2,1)S(1)}, bf16[768,512]{1,0:T(8,128)(2,1)}, f32[768,512]{1,0:T(8,128)S(1)}) custom-call(s32[1]{0:T(128)} %bitcast.1.place_ref, bf16[768,512]{1,0:T(8,128)(2,1)S(1)} %copy-done, bf16[768,512]{1,0:T(8,128)(2,1)S(1)} %copy-done.3, f32[768,1]{1,0:T(8,128)S(1)} %get-tuple-element.37.rate_ref, f32[1536,512]{1,0:T(8,128)} %bitcast.16), custom_call_target="tpu_custom_call" | custom-call | tf_op jit(solution)/shard_map/pallas_call | solution.py:222
  9.6 3.2 %collective-permute-start = (bf16[768,512]{1,0:T(8,128)(2,1)}, bf16[768,512]{1,0:T(8,128)(2,1)S(1)}, u32[]{:S(2)}, u32[]{:S(2)}) collective-permute-start(bf16[768,512]{1,0:T(8,128)(2,1)} %get-tuple-element.16), channel_id=1, source_target_pairs={{0,8},{8,0},{1,9},{9,1},{2,10},{10,2},{3,11},{11,3},{4,12},{12,4},... | collective-permute-start | bytes 2359304 | tf_op jit(solution)/shard_map/ppermute | solution.py:35
  12.9 2.1 %collective-permute-done = bf16[768,512]{1,0:T(8,128)(2,1)S(1)} collective-permute-done((bf16[768,512]{1,0:T(8,128)(2,1)}, bf16[768,512]{1,0:T(8,128)(2,1)S(1)}, u32[]{:S(2)}, u32[]{:S(2)}) %collective-permute-start) | collective-permute-done | bytes 786464 | tf_op jit(solution)/shard_map/ppermute | solution.py:35
  15.9 2.1 %add_convert_fusion.1 = (bf16[384,512]{1,0:T(8,128)(2,1)}, f32[384,512]{1,0:T(8,128)S(1)}) fusion(f32[768,512]{1,0:T(8,128)S(1)} %get-tuple-element.15, s32[]{:T(128)S(6)} %select_n.39, bf16[768,512]{1,0:T(8,128)(2,1)} %copy-done.14, s32[]{:T(128)S(6)} %select_n.37), kind=kLoop, calls=%fused_computation.2 | loop fusion | flops 983040 | bytes 3538952 | tf_op jit(solution)/shard_map/convert_element_type | solution.py:100
  18.7 7.3 %collective-permute-done.1 = bf16[384,512]{1,0:T(8,128)(2,1)S(1)} collective-permute-done((bf16[384,512]{1,0:T(8,128)(2,1)}, bf16[384,512]{1,0:T(8,128)(2,1)S(1)}, u32[]{:S(2)}, u32[]{:S(2)}) %collective-permute-start.1) | collective-permute-done | bytes 393248 | tf_op jit(solution)/shard_map/ppermute | solution.py:35
  27.7 3.0 %collective-permute-start.3 = (bf16[512,512]{1,0:T(8,128)(2,1)}, bf16[512,512]{1,0:T(8,128)(2,1)S(1)}, u32[]{:S(2)}, u32[]{:S(2)}) collective-permute-start(bf16[512,512]{1,0:T(8,128)(2,1)} %slice.12), channel_id=1, source_target_pairs={{0,8},{8,16},{16,24},{24,32},{32,40},{40,48},{48,56},{56,64},{64,7... | collective-permute-start | bytes 1572872 | tf_op jit(solution)/shard_map/ppermute | solution.py:241
  31.6 2.6 %collective-permute-start.4 = (bf16[512,512]{1,0:T(8,128)(2,1)}, bf16[512,512]{1,0:T(8,128)(2,1)S(1)}, u32[]{:S(2)}, u32[]{:S(2)}) collective-permute-start(bf16[512,512]{1,0:T(8,128)(2,1)} %slice.13), channel_id=1, source_target_pairs={{0,8},{8,16},{16,24},{24,32},{32,40},{40,48},{48,56},{56,64},{64,7... | collective-permute-start | bytes 1572872 | tf_op jit(solution)/shard_map/ppermute | solution.py:242
  35.3 5.4 %collective-permute-start.5 = (bf16[192,512]{1,0:T(8,128)(2,1)S(1)}, bf16[192,512]{1,0:T(8,128)(2,1)S(1)}, u32[]{:S(2)}, u32[]{:S(2)}) collective-permute-start(bf16[192,512]{1,0:T(8,128)(2,1)S(1)} %add_convert_fusion.6), channel_id=1, source_target_pairs={{0,64},{8,200},{64,0},{72,136},{128,192},{136,72},{192,128},{200,8... | collective-permute-start | bytes 589832 | tf_op jit(solution)/shard_map/ppermute | solution.py:35
  46.8 2.8 %shard_map.96.attn_ref = f32[768,512]{1,0:T(8,128)S(1)} custom-call(s32[3]{0:T(128)S(1)} %pad_add_fusion.meta_ref, bf16[768,512]{1,0:T(8,128)(2,1)S(1)} %copy-done.1, bf16[512,512]{1,0:T(8,128)(2,1)S(1)} %copy-done.10, bf16[768,512]{1,0:T(8,128)(2,1)S(1)} %copy-done, bf16[512,512]{1,0:T(8,128)(2,1)S(1)} %copy-done.12, bf16[768,512]{1,0:T(8,128)(2,1)S(1)} %copy-done.6), custom_call_target="tpu_custom_call" | custom-call | tf_op jit(solution)/shard_map/pallas_call | solution.py:222
  49.6 3.1 %collective-permute-start.6 = (bf16[192,512]{1,0:T(8,128)(2,1)S(1)}, bf16[192,512]{1,0:T(8,128)(2,1)S(1)}, u32[]{:S(2)}, u32[]{:S(2)}) collective-permute-start(bf16[192,512]{1,0:T(8,128)(2,1)S(1)} %add_convert_fusion.5), channel_id=1, source_target_pairs={{0,192},{8,72},{64,128},{72,8},{128,64},{136,200},{192,0},{200,136... | collective-permute-start | bytes 589832 | tf_op jit(solution)/shard_map/ppermute | solution.py:35
  52.7 5.2 %collective-permute-done.6 = bf16[192,512]{1,0:T(8,128)(2,1)S(1)} collective-permute-done((bf16[192,512]{1,0:T(8,128)(2,1)S(1)}, bf16[192,512]{1,0:T(8,128)(2,1)S(1)}, u32[]{:S(2)}, u32[]{:S(2)}) %collective-permute-start.6) | collective-permute-done | bytes 196640 | tf_op jit(solution)/shard_map/ppermute | solution.py:35
  59.8 24.6 %collective-permute-start.7 = (f32[8,128]{1,0:T(8,128)S(1)}, f32[8,128]{1,0:T(8,128)S(1)}, u32[]{:S(2)}, u32[]{:S(2)}) collective-permute-start(f32[8,128]{1,0:T(8,128)S(1)} %broadcast_in_dim.7), channel_id=1, source_target_pairs={{0,8},{8,0},{1,9},{9,1},{2,10},{10,2},{3,11},{11,3},{4,12},{12,4},... | collective-permute-start | bytes 12296 | tf_op jit(solution)/shard_map/ppermute | solution.py:35
  86.0 3.0 %collective-permute-start.9 = (f32[8,128]{1,0:T(8,128)S(1)}, f32[8,128]{1,0:T(8,128)S(1)}, u32[]{:S(2)}, u32[]{:S(2)}) collective-permute-start(f32[8,128]{1,0:T(8,128)S(1)} %broadcast_add_fusion.1), channel_id=1, source_target_pairs={{0,4},{1,5},{2,6},{3,7},{4,0},{5,1},{6,2},{7,3},{8,12},{9,13},{10,... | collective-permute-start | bytes 12296 | tf_op jit(solution)/shard_map/ppermute | solution.py:35
  90.0 2.6 %collective-permute-done.10 = f32[8,128]{1,0:T(8,128)S(1)} collective-permute-done((f32[8,128]{1,0:T(8,128)S(1)}, f32[8,128]{1,0:T(8,128)S(1)}, u32[]{:S(2)}, u32[]{:S(2)}) %collective-permute-start.10) | collective-permute-done | bytes 4128 | tf_op jit(solution)/shard_map/ppermute | solution.py:35
  93.8 2.9 %collective-permute-start.11 = (f32[8,128]{1,0:T(8,128)S(1)}, f32[8,128]{1,0:T(8,128)}, u32[]{:S(2)}, u32[]{:S(2)}) collective-permute-start(f32[8,128]{1,0:T(8,128)S(1)} %add_add_fusion.3), channel_id=1, source_target_pairs={{0,16},{16,0},{32,48},{48,32},{1,17},{17,1},{33,49},{49,33},{2,18}... | collective-permute-start | bytes 12296 | tf_op jit(solution)/shard_map/ppermute | solution.py:35
  97.3 2.6 %collective-permute-start.18 = (bf16[192,512]{1,0:T(8,128)(2,1)}, bf16[192,512]{1,0:T(8,128)(2,1)S(1)}, u32[]{:S(2)}, u32[]{:S(2)}) collective-permute-start(bf16[192,512]{1,0:T(8,128)(2,1)} %get-tuple-element.34.rest_0_), channel_id=1, source_target_pairs={{0,8},{8,0},{1,9},{9,1},{2,10},{10,2},{3,11},{11,3},{4,12},{12,4},... | collective-permute-start | bytes 589832 | tf_op jit(solution)/shard_map/ppermute | solution.py:35
  99.9 2.7 %collective-permute-start.17 = (bf16[192,512]{1,0:T(8,128)(2,1)}, bf16[192,512]{1,0:T(8,128)(2,1)S(1)}, u32[]{:S(2)}, u32[]{:S(2)}) collective-permute-start(bf16[192,512]{1,0:T(8,128)(2,1)} %collective-permute-done.15.rest_1_), channel_id=1, source_target_pairs={{0,16},{8,56},{16,0},{24,40},{32,48},{40,24},{48,32},{56,8},{1,17}... | collective-permute-start | bytes 589832 | tf_op jit(solution)/shard_map/ppermute | solution.py:35
  104.0 1.8 %collective-permute-done.16.rest_2_ = bf16[192,512]{1,0:T(8,128)(2,1)S(1)} collective-permute-done((bf16[192,512]{1,0:T(8,128)(2,1)}, bf16[192,512]{1,0:T(8,128)(2,1)S(1)}, u32[]{:S(2)}, u32[]{:S(2)}) %collective-permute-start.16) | collective-permute-done | bytes 196640 | tf_op jit(solution)/shard_map/ppermute | solution.py:35
  105.9 2.1 %collective-permute-done.17.rest_3_ = bf16[192,512]{1,0:T(8,128)(2,1)S(1)} collective-permute-done((bf16[192,512]{1,0:T(8,128)(2,1)}, bf16[192,512]{1,0:T(8,128)(2,1)S(1)}, u32[]{:S(2)}, u32[]{:S(2)}) %collective-permute-start.17) | collective-permute-done | bytes 196640 | tf_op jit(solution)/shard_map/ppermute | solution.py:35
  110.5 7.8 %shard_map.97 = (f32[1536,512]{1,0:T(8,128)}, bf16[1536,512]{1,0:T(8,128)(2,1)S(1)}, bf16[768,512]{1,0:T(8,128)(2,1)S(1)}, f32[768,512]{1,0:T(8,128)}) custom-call(s32[1]{0:T(128)} %bitcast.1.place_ref, s32[8]{0:T(128)S(1)} %broadcast_multiply_fusion.starts_ref, f32[1]{0:T(128)} %bitcast.12.square_ref, bf16[768,512]{1,0:T(8,128)(2,1)S(1)} %copy-done, ...), custom_call_target="tpu_custom_call" | custom-call | tf_op jit(solution)/shard_map/pallas_call | solution.py:222
  118.6 2.0 %collective-permute-done.22 = bf16[768,512]{1,0:T(8,128)(2,1)S(1)} collective-permute-done((bf16[768,512]{1,0:T(8,128)(2,1)S(1)}, bf16[768,512]{1,0:T(8,128)(2,1)S(1)}, u32[]{:S(2)}, u32[]{:S(2)}) %collective-permute-start.22) | collective-permute-done | bytes 786464 | tf_op jit(solution)/shard_map/ppermute | solution.py:35
  123.0 7.3 %collective-permute-done.23 = bf16[384,512]{1,0:T(8,128)(2,1)S(1)} collective-permute-done((bf16[384,512]{1,0:T(8,128)(2,1)S(1)}, bf16[384,512]{1,0:T(8,128)(2,1)S(1)}, u32[]{:S(2)}, u32[]{:S(2)}) %collective-permute-start.23) | collective-permute-done | bytes 393248 | tf_op jit(solution)/shard_map/ppermute | solution.py:35
  130.4 4.8 %collective-permute-done.24 = bf16[192,512]{1,0:T(8,128)(2,1)S(1)} collective-permute-done((bf16[192,512]{1,0:T(8,128)(2,1)S(1)}, bf16[192,512]{1,0:T(8,128)(2,1)S(1)}, u32[]{:S(2)}, u32[]{:S(2)}) %collective-permute-start.24) | collective-permute-done | bytes 196640 | tf_op jit(solution)/shard_map/ppermute | solution.py:35
  135.2 4.4 %collective-permute-start.25 = (bf16[192,512]{1,0:T(8,128)(2,1)S(1)}, bf16[192,512]{1,0:T(8,128)(2,1)S(1)}, u32[]{:S(2)}, u32[]{:S(2)}) collective-permute-start(bf16[192,512]{1,0:T(8,128)(2,1)S(1)} %add_convert_fusion.3), channel_id=1, source_target_pairs={{0,64},{8,200},{64,0},{72,136},{128,192},{136,72},{192,128},{200,8... | collective-permute-start | bytes 589832 | tf_op jit(solution)/shard_map/ppermute | solution.py:35
  139.7 4.2 %shard_map.98 = bf16[768,512]{1,0:T(8,128)(2,1)} custom-call(s32[3]{0:T(128)S(1)} %pad_add_fusion.meta_ref, bf16[768,512]{1,0:T(8,128)(2,1)S(1)} %copy-done.1, f32[768,512]{1,0:T(8,128)S(1)} %shard_map.96.attn_ref, bf16[1536,512]{1,0:T(8,128)(2,1)S(1)} %copy-done.8, bf16[1536,512]{1,0:T(8,128)(2,1)S(1)} %get-tuple-element.24.late_ref), custom_call_target="tpu_custom_call" | custom-call | tf_op jit(solution)/shard_map/pallas_call | solution.py:222
  145.0 7.3 %collective-permute-done.26 = bf16[192,512]{1,0:T(8,128)(2,1)S(1)} collective-permute-done((bf16[192,512]{1,0:T(8,128)(2,1)S(1)}, bf16[192,512]{1,0:T(8,128)(2,1)S(1)}, u32[]{:S(2)}, u32[]{:S(2)}) %collective-permute-start.26) | collective-permute-done | bytes 196640 | tf_op jit(solution)/shard_map/ppermute | solution.py:35
  153.8 1.9 %collective-permute-start.27 = (f32[8,128]{1,0:T(8,128)S(1)}, f32[8,128]{1,0:T(8,128)S(1)}, u32[]{:S(2)}, u32[]{:S(2)}) collective-permute-start(f32[8,128]{1,0:T(8,128)S(1)} %broadcast_in_dim.8), channel_id=1, source_target_pairs={{0,8},{8,0},{1,9},{9,1},{2,10},{10,2},{3,11},{11,3},{4,12},{12,4},... | collective-permute-start | bytes 12296 | tf_op jit(solution)/shard_map/ppermute | solution.py:35
  160.7 2.0 %collective-permute-start.37 = (bf16[192,512]{1,0:T(8,128)(2,1)S(1)}, bf16[192,512]{1,0:T(8,128)(2,1)S(1)}, u32[]{:S(2)}, u32[]{:S(2)}) collective-permute-start(bf16[192,512]{1,0:T(8,128)(2,1)S(1)} %collective-permute-done.35.rest_1_), channel_id=1, source_target_pairs={{0,16},{8,56},{16,0},{24,40},{32,48},{40,24},{48,32},{56,8},{1,17}... | collective-permute-start | bytes 589832 | tf_op jit(solution)/shard_map/ppermute | solution.py:35
  167.8 2.3 %collective-permute-start.38 = (bf16[192,512]{1,0:T(8,128)(2,1)S(1)}, bf16[192,512]{1,0:T(8,128)(2,1)S(1)}, u32[]{:S(2)}, u32[]{:S(2)}) collective-permute-start(bf16[192,512]{1,0:T(8,128)(2,1)S(1)} %get-tuple-element.32.rest_0_), channel_id=1, source_target_pairs={{0,8},{8,0},{1,9},{9,1},{2,10},{10,2},{3,11},{11,3},{4,12},{12,4},... | collective-permute-start | bytes 589832 | tf_op jit(solution)/shard_map/ppermute | solution.py:35
  170.1 1.9 %collective-permute-start.39 = (bf16[192,512]{1,0:T(8,128)(2,1)S(1)}, bf16[192,512]{1,0:T(8,128)(2,1)S(1)}, u32[]{:S(2)}, u32[]{:S(2)}) collective-permute-start(bf16[192,512]{1,0:T(8,128)(2,1)S(1)} %collective-permute-done.35.rest_1_), channel_id=1, source_target_pairs={{0,8},{8,0},{1,9},{9,1},{2,10},{10,2},{3,11},{11,3},{4,12},{12,4},... | collective-permute-start | bytes 589832 | tf_op jit(solution)/shard_map/ppermute | solution.py:35
  172.7 2.5 %collective-permute-done.34 = f32[8,128]{1,0:T(8,128)S(1)} collective-permute-done((f32[8,128]{1,0:T(8,128)S(1)}, f32[8,128]{1,0:T(8,128)S(1)}, u32[]{:S(2)}, u32[]{:S(2)}) %collective-permute-start.34) | collective-permute-done | bytes 4128 | tf_op jit(solution)/shard_map/ppermute | solution.py:35
  175.7 3.2 %shard_map.99 = f32[1536,512]{1,0:T(8,128)} custom-call(s32[8]{0:T(128)S(1)} %broadcast_multiply_fusion.starts_ref, f32[1]{0:T(128)} %bitcast.13.square_ref, f32[1536,512]{1,0:T(8,128)S(1)} %copy-done.2, bf16[192,512]{1,0:T(8,128)(2,1)S(1)} %get-tuple-element.32.rest_0_, bf16[192,512]{1,0:T(8,128)(2,1)S(1)} %collective-permute-done.35.rest_1_, ...), custom_call_target="tpu_custom_call" | custom-call | tf_op jit(solution)/shard_map/pallas_call | solution.py:222
  (118 shorter events, 39.8 us)
Async XLA Ops:
  9.6 5.4 %collective-permute-start = (bf16[768,512]{1,0:T(8,128)(2,1)}, bf16[768,512]{1,0:T(8,128)(2,1)S(1)}, u32[]{:S(2)}, u32[]{:S(2)}) collective-permute-start(bf16[768,512]{1,0:T(8,128)(2,1)} %get-tuple-element.16), channel_id=1, source_target_pairs={{0,8},{8,0},{1,9},{9,1},{2,10},{10,2},{3,11},{11,3},{4,12},{12,4},... | collective-permute-start | bytes 2359304 | tf_op jit(solution)/shard_map/ppermute | solution.py:35
  18.0 8.0 %collective-permute-start.1 = (bf16[384,512]{1,0:T(8,128)(2,1)}, bf16[384,512]{1,0:T(8,128)(2,1)S(1)}, u32[]{:S(2)}, u32[]{:S(2)}) collective-permute-start(bf16[384,512]{1,0:T(8,128)(2,1)} %get-tuple-element.30), channel_id=1, source_target_pairs={{0,16},{8,56},{16,0},{24,40},{32,48},{40,24},{48,32},{56,8},{1,17}... | collective-permute-start | bytes 1179656 | tf_op jit(solution)/shard_map/ppermute | solution.py:35
  26.8 7.4 %collective-permute-start.2 = (bf16[192,512]{1,0:T(8,128)(2,1)}, bf16[192,512]{1,0:T(8,128)(2,1)S(1)}, u32[]{:S(2)}, u32[]{:S(2)}) collective-permute-start(bf16[192,512]{1,0:T(8,128)(2,1)} %add_convert_fusion.7), channel_id=1, source_target_pairs={{0,48},{8,24},{16,32},{24,8},{32,16},{40,56},{48,0},{56,40},{1,49}... | collective-permute-start | bytes 589832 | tf_op jit(solution)/shard_map/ppermute | solution.py:35
  27.7 13.8 %collective-permute-start.3 = (bf16[512,512]{1,0:T(8,128)(2,1)}, bf16[512,512]{1,0:T(8,128)(2,1)S(1)}, u32[]{:S(2)}, u32[]{:S(2)}) collective-permute-start(bf16[512,512]{1,0:T(8,128)(2,1)} %slice.12), channel_id=1, source_target_pairs={{0,8},{8,16},{16,24},{24,32},{32,40},{40,48},{48,56},{56,64},{64,7... | collective-permute-start | bytes 1572872 | tf_op jit(solution)/shard_map/ppermute | solution.py:241
  31.6 11.2 %collective-permute-start.4 = (bf16[512,512]{1,0:T(8,128)(2,1)}, bf16[512,512]{1,0:T(8,128)(2,1)S(1)}, u32[]{:S(2)}, u32[]{:S(2)}) collective-permute-start(bf16[512,512]{1,0:T(8,128)(2,1)} %slice.13), channel_id=1, source_target_pairs={{0,8},{8,16},{16,24},{24,32},{32,40},{40,48},{48,56},{56,64},{64,7... | collective-permute-start | bytes 1572872 | tf_op jit(solution)/shard_map/ppermute | solution.py:242
  35.3 14.2 %collective-permute-start.5 = (bf16[192,512]{1,0:T(8,128)(2,1)S(1)}, bf16[192,512]{1,0:T(8,128)(2,1)S(1)}, u32[]{:S(2)}, u32[]{:S(2)}) collective-permute-start(bf16[192,512]{1,0:T(8,128)(2,1)S(1)} %add_convert_fusion.6), channel_id=1, source_target_pairs={{0,64},{8,200},{64,0},{72,136},{128,192},{136,72},{192,128},{200,8... | collective-permute-start | bytes 589832 | tf_op jit(solution)/shard_map/ppermute | solution.py:35
  49.6 8.2 %collective-permute-start.6 = (bf16[192,512]{1,0:T(8,128)(2,1)S(1)}, bf16[192,512]{1,0:T(8,128)(2,1)S(1)}, u32[]{:S(2)}, u32[]{:S(2)}) collective-permute-start(bf16[192,512]{1,0:T(8,128)(2,1)S(1)} %add_convert_fusion.5), channel_id=1, source_target_pairs={{0,192},{8,72},{64,128},{72,8},{128,64},{136,200},{192,0},{200,136... | collective-permute-start | bytes 589832 | tf_op jit(solution)/shard_map/ppermute | solution.py:35
  59.8 25.5 %collective-permute-start.7 = (f32[8,128]{1,0:T(8,128)S(1)}, f32[8,128]{1,0:T(8,128)S(1)}, u32[]{:S(2)}, u32[]{:S(2)}) collective-permute-start(f32[8,128]{1,0:T(8,128)S(1)} %broadcast_in_dim.7), channel_id=1, source_target_pairs={{0,8},{8,0},{1,9},{9,1},{2,10},{10,2},{3,11},{11,3},{4,12},{12,4},... | collective-permute-start | bytes 12296 | tf_op jit(solution)/shard_map/ppermute | solution.py:35
  86.0 4.0 %collective-permute-start.9 = (f32[8,128]{1,0:T(8,128)S(1)}, f32[8,128]{1,0:T(8,128)S(1)}, u32[]{:S(2)}, u32[]{:S(2)}) collective-permute-start(f32[8,128]{1,0:T(8,128)S(1)} %broadcast_add_fusion.1), channel_id=1, source_target_pairs={{0,4},{1,5},{2,6},{3,7},{4,0},{5,1},{6,2},{7,3},{8,12},{9,13},{10,... | collective-permute-start | bytes 12296 | tf_op jit(solution)/shard_map/ppermute | solution.py:35
  89.8 10.1 %collective-permute-start.15 = (bf16[192,512]{1,0:T(8,128)(2,1)}, bf16[192,512]{1,0:T(8,128)(2,1)}, u32[]{:S(2)}, u32[]{:S(2)}) collective-permute-start(bf16[192,512]{1,0:T(8,128)(2,1)} %get-tuple-element.34.rest_0_), channel_id=1, source_target_pairs={{0,48},{8,24},{16,32},{24,8},{32,16},{40,56},{48,0},{56,40},{1,49}... | collective-permute-start | bytes 589832 | tf_op jit(solution)/shard_map/ppermute | solution.py:35
  93.3 6.6 %collective-permute-start.13 = (f32[8,128]{1,0:T(8,128)S(1)}, f32[8,128]{1,0:T(8,128)S(1)}, u32[]{:S(2)}, u32[]{:S(2)}) collective-permute-start(f32[8,128]{1,0:T(8,128)S(1)} %add_add_fusion.3), channel_id=1, source_target_pairs={{0,48},{16,32},{32,16},{48,0},{1,49},{17,33},{33,17},{49,1},{2,50}... | collective-permute-start | bytes 12296 | tf_op jit(solution)/shard_map/ppermute | solution.py:35
  93.4 9.2 %collective-permute-start.12 = (f32[8,128]{1,0:T(8,128)S(1)}, f32[8,128]{1,0:T(8,128)S(1)}, u32[]{:S(2)}, u32[]{:S(2)}) collective-permute-start(f32[8,128]{1,0:T(8,128)S(1)} %add_add_fusion.3), channel_id=1, source_target_pairs={{0,32},{16,48},{32,0},{48,16},{1,33},{17,49},{33,1},{49,17},{2,34}... | collective-permute-start | bytes 12296 | tf_op jit(solution)/shard_map/ppermute | solution.py:35
  93.8 8.8 %collective-permute-start.11 = (f32[8,128]{1,0:T(8,128)S(1)}, f32[8,128]{1,0:T(8,128)}, u32[]{:S(2)}, u32[]{:S(2)}) collective-permute-start(f32[8,128]{1,0:T(8,128)S(1)} %add_add_fusion.3), channel_id=1, source_target_pairs={{0,16},{16,0},{32,48},{48,32},{1,17},{17,1},{33,49},{49,33},{2,18}... | collective-permute-start | bytes 12296 | tf_op jit(solution)/shard_map/ppermute | solution.py:35
  97.3 11.9 %collective-permute-start.18 = (bf16[192,512]{1,0:T(8,128)(2,1)}, bf16[192,512]{1,0:T(8,128)(2,1)S(1)}, u32[]{:S(2)}, u32[]{:S(2)}) collective-permute-start(bf16[192,512]{1,0:T(8,128)(2,1)} %get-tuple-element.34.rest_0_), channel_id=1, source_target_pairs={{0,8},{8,0},{1,9},{9,1},{2,10},{10,2},{3,11},{11,3},{4,12},{12,4},... | collective-permute-start | bytes 589832 | tf_op jit(solution)/shard_map/ppermute | solution.py:35
  99.9 5.9 %collective-permute-start.16 = (bf16[192,512]{1,0:T(8,128)(2,1)}, bf16[192,512]{1,0:T(8,128)(2,1)S(1)}, u32[]{:S(2)}, u32[]{:S(2)}) collective-permute-start(bf16[192,512]{1,0:T(8,128)(2,1)} %get-tuple-element.34.rest_0_), channel_id=1, source_target_pairs={{0,16},{8,56},{16,0},{24,40},{32,48},{40,24},{48,32},{56,8},{1,17}... | collective-permute-start | bytes 589832 | tf_op jit(solution)/shard_map/ppermute | solution.py:35
  99.9 8.0 %collective-permute-start.17 = (bf16[192,512]{1,0:T(8,128)(2,1)}, bf16[192,512]{1,0:T(8,128)(2,1)S(1)}, u32[]{:S(2)}, u32[]{:S(2)}) collective-permute-start(bf16[192,512]{1,0:T(8,128)(2,1)} %collective-permute-done.15.rest_1_), channel_id=1, source_target_pairs={{0,16},{8,56},{16,0},{24,40},{32,48},{40,24},{48,32},{56,8},{1,17}... | collective-permute-start | bytes 589832 | tf_op jit(solution)/shard_map/ppermute | solution.py:35
  103.2 5.3 %collective-permute-start.14 = (f32[8,128]{1,0:T(8,128)S(1)}, f32[8,128]{1,0:T(8,128)S(1)}, u32[]{:S(2)}, u32[]{:S(2)}) collective-permute-start(f32[8,128]{1,0:T(8,128)S(1)} %add_add_fusion.2), channel_id=1, source_target_pairs={{0,1},{1,0},{2,3},{3,2},{4,5},{5,4},{6,7},{7,6},{8,9},{9,8},{10,11... | collective-permute-start | bytes 12296 | tf_op jit(solution)/shard_map/ppermute | solution.py:35
  104.0 5.1 %collective-permute-start.19 = (bf16[192,512]{1,0:T(8,128)(2,1)}, bf16[192,512]{1,0:T(8,128)(2,1)S(1)}, u32[]{:S(2)}, u32[]{:S(2)}) collective-permute-start(bf16[192,512]{1,0:T(8,128)(2,1)} %collective-permute-done.15.rest_1_), channel_id=1, source_target_pairs={{0,8},{8,0},{1,9},{9,1},{2,10},{10,2},{3,11},{11,3},{4,12},{12,4},... | collective-permute-start | bytes 589832 | tf_op jit(solution)/shard_map/ppermute | solution.py:35
  122.3 7.9 %collective-permute-start.23 = (bf16[384,512]{1,0:T(8,128)(2,1)S(1)}, bf16[384,512]{1,0:T(8,128)(2,1)S(1)}, u32[]{:S(2)}, u32[]{:S(2)}) collective-permute-start(bf16[384,512]{1,0:T(8,128)(2,1)S(1)} %get-tuple-element.28), channel_id=1, source_target_pairs={{0,16},{8,56},{16,0},{24,40},{32,48},{40,24},{48,32},{56,8},{1,17}... | collective-permute-start | bytes 1179656 | tf_op jit(solution)/shard_map/ppermute | solution.py:35
  130.3 4.9 %collective-permute-start.24 = (bf16[192,512]{1,0:T(8,128)(2,1)S(1)}, bf16[192,512]{1,0:T(8,128)(2,1)S(1)}, u32[]{:S(2)}, u32[]{:S(2)}) collective-permute-start(bf16[192,512]{1,0:T(8,128)(2,1)S(1)} %add_convert_fusion.4), channel_id=1, source_target_pairs={{0,48},{8,24},{16,32},{24,8},{32,16},{40,56},{48,0},{56,40},{1,49}... | collective-permute-start | bytes 589832 | tf_op jit(solution)/shard_map/ppermute | solution.py:35
  135.2 9.6 %collective-permute-start.25 = (bf16[192,512]{1,0:T(8,128)(2,1)S(1)}, bf16[192,512]{1,0:T(8,128)(2,1)S(1)}, u32[]{:S(2)}, u32[]{:S(2)}) collective-permute-start(bf16[192,512]{1,0:T(8,128)(2,1)S(1)} %add_convert_fusion.3), channel_id=1, source_target_pairs={{0,64},{8,200},{64,0},{72,136},{128,192},{136,72},{192,128},{200,8... | collective-permute-start | bytes 589832 | tf_op jit(solution)/shard_map/ppermute | solution.py:35
  144.9 7.4 %collective-permute-start.26 = (bf16[192,512]{1,0:T(8,128)(2,1)S(1)}, bf16[192,512]{1,0:T(8,128)(2,1)S(1)}, u32[]{:S(2)}, u32[]{:S(2)}) collective-permute-start(bf16[192,512]{1,0:T(8,128)(2,1)S(1)} %add_convert_fusion.2), channel_id=1, source_target_pairs={{0,192},{8,72},{64,128},{72,8},{128,64},{136,200},{192,0},{200,136... | collective-permute-start | bytes 589832 | tf_op jit(solution)/shard_map/ppermute | solution.py:35
  155.7 4.9 %collective-permute-start.35 = (bf16[192,512]{1,0:T(8,128)(2,1)S(1)}, bf16[192,512]{1,0:T(8,128)(2,1)S(1)}, u32[]{:S(2)}, u32[]{:S(2)}) collective-permute-start(bf16[192,512]{1,0:T(8,128)(2,1)S(1)} %get-tuple-element.32.rest_0_), channel_id=1, source_target_pairs={{0,48},{8,24},{16,32},{24,8},{32,16},{40,56},{48,0},{56,40},{1,49}... | collective-permute-start | bytes 589832 | tf_op jit(solution)/shard_map/ppermute | solution.py:35
  157.2 5.4 %collective-permute-start.29 = (f32[8,128]{1,0:T(8,128)S(1)}, f32[8,128]{1,0:T(8,128)S(1)}, u32[]{:S(2)}, u32[]{:S(2)}) collective-permute-start(f32[8,128]{1,0:T(8,128)S(1)} %broadcast_add_fusion), channel_id=1, source_target_pairs={{0,4},{1,5},{2,6},{3,7},{4,0},{5,1},{6,2},{7,3},{8,12},{9,13},{10,... | collective-permute-start | bytes 12296 | tf_op jit(solution)/shard_map/ppermute | solution.py:35
  158.5 4.1 %collective-permute-start.30 = (f32[8,128]{1,0:T(8,128)S(1)}, f32[8,128]{1,0:T(8,128)S(1)}, u32[]{:S(2)}, u32[]{:S(2)}) collective-permute-start(f32[8,128]{1,0:T(8,128)S(1)} %broadcast_add_fusion), channel_id=1, source_target_pairs={{0,6},{1,7},{2,4},{3,5},{4,2},{5,3},{6,0},{7,1},{8,14},{9,15},{10,... | collective-permute-start | bytes 12296 | tf_op jit(solution)/shard_map/ppermute | solution.py:35
  159.9 12.1 %collective-permute-start.36 = (bf16[192,512]{1,0:T(8,128)(2,1)S(1)}, bf16[192,512]{1,0:T(8,128)(2,1)S(1)}, u32[]{:S(2)}, u32[]{:S(2)}) collective-permute-start(bf16[192,512]{1,0:T(8,128)(2,1)S(1)} %get-tuple-element.32.rest_0_), channel_id=1, source_target_pairs={{0,16},{8,56},{16,0},{24,40},{32,48},{40,24},{48,32},{56,8},{1,17}... | collective-permute-start | bytes 589832 | tf_op jit(solution)/shard_map/ppermute | solution.py:35
  160.7 11.4 %collective-permute-start.37 = (bf16[192,512]{1,0:T(8,128)(2,1)S(1)}, bf16[192,512]{1,0:T(8,128)(2,1)S(1)}, u32[]{:S(2)}, u32[]{:S(2)}) collective-permute-start(bf16[192,512]{1,0:T(8,128)(2,1)S(1)} %collective-permute-done.35.rest_1_), channel_id=1, source_target_pairs={{0,16},{8,56},{16,0},{24,40},{32,48},{40,24},{48,32},{56,8},{1,17}... | collective-permute-start | bytes 589832 | tf_op jit(solution)/shard_map/ppermute | solution.py:35
  163.3 4.5 %collective-permute-start.33 = (f32[8,128]{1,0:T(8,128)S(1)}, f32[8,128]{1,0:T(8,128)S(1)}, u32[]{:S(2)}, u32[]{:S(2)}) collective-permute-start(f32[8,128]{1,0:T(8,128)S(1)} %add_add_fusion.1), channel_id=1, source_target_pairs={{0,48},{16,32},{32,16},{48,0},{1,49},{17,33},{33,17},{49,1},{2,50}... | collective-permute-start | bytes 12296 | tf_op jit(solution)/shard_map/ppermute | solution.py:35
  164.6 5.5 %collective-permute-start.32 = (f32[8,128]{1,0:T(8,128)S(1)}, f32[8,128]{1,0:T(8,128)S(1)}, u32[]{:S(2)}, u32[]{:S(2)}) collective-permute-start(f32[8,128]{1,0:T(8,128)S(1)} %add_add_fusion.1), channel_id=1, source_target_pairs={{0,32},{16,48},{32,0},{48,16},{1,33},{17,49},{33,1},{49,17},{2,34}... | collective-permute-start | bytes 12296 | tf_op jit(solution)/shard_map/ppermute | solution.py:35
  165.4 7.1 %collective-permute-start.31 = (f32[8,128]{1,0:T(8,128)S(1)}, f32[8,128]{1,0:T(8,128)S(1)}, u32[]{:S(2)}, u32[]{:S(2)}) collective-permute-start(f32[8,128]{1,0:T(8,128)S(1)} %add_add_fusion.1), channel_id=1, source_target_pairs={{0,16},{16,0},{32,48},{48,32},{1,17},{17,1},{33,49},{49,33},{2,18}... | collective-permute-start | bytes 12296 | tf_op jit(solution)/shard_map/ppermute | solution.py:35
  167.8 7.9 %collective-permute-start.38 = (bf16[192,512]{1,0:T(8,128)(2,1)S(1)}, bf16[192,512]{1,0:T(8,128)(2,1)S(1)}, u32[]{:S(2)}, u32[]{:S(2)}) collective-permute-start(bf16[192,512]{1,0:T(8,128)(2,1)S(1)} %get-tuple-element.32.rest_0_), channel_id=1, source_target_pairs={{0,8},{8,0},{1,9},{9,1},{2,10},{10,2},{3,11},{11,3},{4,12},{12,4},... | collective-permute-start | bytes 589832 | tf_op jit(solution)/shard_map/ppermute | solution.py:35
  170.1 5.6 %collective-permute-start.39 = (bf16[192,512]{1,0:T(8,128)(2,1)S(1)}, bf16[192,512]{1,0:T(8,128)(2,1)S(1)}, u32[]{:S(2)}, u32[]{:S(2)}) collective-permute-start(bf16[192,512]{1,0:T(8,128)(2,1)S(1)} %collective-permute-done.35.rest_1_), channel_id=1, source_target_pairs={{0,8},{8,0},{1,9},{9,1},{2,10},{10,2},{3,11},{11,3},{4,12},{12,4},... | collective-permute-start | bytes 589832 | tf_op jit(solution)/shard_map/ppermute | solution.py:35
  (26 other events, 132.9 us)
